TPU v7x, 128 devices: a whole 4x4x4 slice. The times are simulated.
128 devices in a mesh: lon: 8 (over z_hi, x), lat: 16 (over z_lo, y, core).
Axes of the slice: x: 4, y: 4, z: 4 (z_hi: 2, z_lo: 2; z = z_hi * 2 + z_lo), core: 2. Of those that a mesh axis runs over, the one named last changes fastest.
Arguments:
- tracers: float32 [2, 16, 512, 1024], P(None, None, 'lat', 'lon'), may hold values from -6 to 6
- velocity: float32 [2, 16, 512, 1024], P(None, None, 'lat', 'lon'), may hold values from -3 to 3
- land_mask: int32 [512, 1024], P('lat', 'lon'), may hold values 0 or 1
- mixing: float32 [512, 1024], P('lat', 'lon'), may hold values from 0.05 to 0.25
- owners: int32 [4096, 1], P(('lon', 'lat')), may hold values from 0 to 127; in each aligned block of 32 rows (0 to 31, 32 to 63, ...) at most 2 rows name the same one
- atm_row: int32 [4096], P(('lon', 'lat')), may hold values from 0 to 31
Outputs:
- tracers_out: float32 [2, 16, 512, 1024], P(None, None, 'lat', 'lon')
- velocity_out: float32 [2, 16, 512, 1024], P(None, None, 'lat', 'lon')
- atm_surface: float32 [4, 4096, 128], P(None, ('lon', 'lat'))
- atm_cover: float32 [4096, 128], P(('lon', 'lat'))
Inputs may be any that keep to these rules, and one draw needn't show every extreme that they name: `owners`: among the 32 blocks of one device at most 2 name the same owner, and in every draw some owner is named by exactly 2 blocks of some device.
All inputs are finite; a program needn't handle non-finite values. No bound on the sum of `land_mask` on one device may be relied on, other than what follows from the above.
Results may differ from a plain program's by a relative error of at most 0.00007.
Values sent between devices are 32-bit elements; how exact they have to be, the bound alone decides.
A program may use at most 64 MiB of HBM per device.

v0:
```python
import math

import jax
import jax.numpy as jnp
from jax import lax
from jax.sharding import PartitionSpec as P

STEPS = 2
ATM_ROWS = 32


THERMAL = 0.2
HALINE = 0.15
GRAVITY = 0.2
TIMESTEP = 0.8
VERTICAL_MIX = 0.1
VISCOSITY = 0.2
CORIOLIS_MAX = 0.3


def extended(shard, sides, width, wrap):
    for axis, dim in sides:
        count, length = (lax.axis_size(axis), shard.shape[dim])
        up = [(i, (i + 1) % count) for i in range(count if wrap else count - 1)]
        down = [(j, i) for i, j in up]
        last = lax.slice_in_dim(shard, length - width, length, axis=dim)
        leading = lax.slice_in_dim(shard, 0, width, axis=dim)
        before = lax.ppermute(last, axis, up)
        after = lax.ppermute(leading, axis, down)
        shard = jnp.concatenate([before, shard, after], axis=dim)
    return shard


def from_partner(shard, axis, distance):
    return lax.ppermute(shard, axis, [(i, i ^ 1 << distance) for i in range(lax.axis_size(axis))])


def in_blocks(shard, dim, count):
    lengths = shard.shape
    pieces = shard.reshape(*lengths[:dim], count, lengths[dim] // count, *lengths[dim + 1 :])
    return jnp.moveaxis(pieces, dim, 0)


def in_order(pieces, dim):
    pieces = jnp.moveaxis(pieces, 0, dim)
    lengths = pieces.shape
    return pieces.reshape(*lengths[:dim], lengths[dim] * lengths[dim + 1], *lengths[dim + 2 :])


def exchange_both(shard, axis, axes, splits, concats):
    sizes = [lax.axis_size(a) for a in axes]
    pieces = in_blocks(shard, splits[0], sizes[0])
    pieces = jnp.moveaxis(in_blocks(pieces, splits[1] + 1, sizes[1]), 0, 1)
    inside = pieces.shape[2:]
    pieces = pieces.reshape(-1, *inside)
    pieces = lax.all_to_all(pieces, axis, split_axis=0, concat_axis=0, tiled=True)
    pieces = in_order(pieces.reshape(*sizes, *inside), concats[0] + 1)
    return in_order(pieces, concats[1])


def pressure(fields):
    density = HALINE * fields[1] - THERMAL * fields[0]
    return GRAVITY * (jnp.cumsum(density, axis=0) - 0.5 * density)


def coriolis_table(latitude, total_rows):
    return CORIOLIS_MAX * jnp.sin(math.pi * (-0.43 + 0.93 * (latitude + 0.5) / total_rows))


def neighbour(center, edge_value, axis, shift, position):
    rolled = jnp.roll(center, shift, axis=axis)
    return jnp.where(position, jnp.expand_dims(edge_value, axis), rolled)


def level_shift(fields, shift, at_end):
    rolled = jnp.roll(fields, shift, axis=1)
    return jnp.where(at_end, fields, rolled)


def local(tracers, velocity, land_mask, mixing, owners, atm_row):
    wet_mask = land_mask.astype(jnp.float32)
    levels = tracers.shape[1]
    rows_local, cols_local = land_mask.shape
    field_rows = jnp.concatenate(
        [
            (tracers * wet_mask).reshape(2 * levels, rows_local, cols_local),
            (velocity * wet_mask).reshape(2 * levels, rows_local, cols_local),
        ],
        axis=0,
    )
    sign_rows = jnp.concatenate(
        [
            jnp.ones((2 * levels,), jnp.float32),
            -jnp.ones((2 * levels,), jnp.float32),
            jnp.ones((1,), jnp.float32),
        ]
    )[:, None]
    lat_count = lax.axis_size("lat")
    lon_count = lax.axis_size("lon")
    lat_index = lax.axis_index("lat")
    latitude = (lat_index * rows_local + jnp.arange(rows_local)).astype(jnp.float32)
    coriolis = coriolis_table(latitude, lat_count * rows_local)[:, None]
    is_top = lat_index == lat_count - 1
    bit_total = lon_count.bit_length() - 1
    column_id = jnp.arange(cols_local, dtype=jnp.int32)[None, :]
    row_id = jnp.arange(rows_local, dtype=jnp.int32)[:, None]
    first_col = column_id == 0
    last_col = column_id == cols_local - 1
    first_row = row_id == 0
    last_row = row_id == rows_local - 1
    level_id = jnp.arange(levels, dtype=jnp.int32)[None, :, None, None]
    top_level = level_id == 0
    bottom_level = level_id == levels - 1
    for step_index in range(STEPS):
        col_edges = jnp.concatenate(
            [
                jnp.concatenate([field_rows[:, :, :1], field_rows[:, :, -1:]], axis=2),
                jnp.stack([wet_mask[:, 0], wet_mask[:, -1]], axis=1)[None],
            ],
            axis=0,
        )
        row_edges = jnp.concatenate(
            [
                jnp.stack([field_rows[:, 0, :], field_rows[:, -1, :]], axis=1),
                jnp.stack([wet_mask[0], wet_mask[-1]], axis=0)[None],
            ],
            axis=0,
        )
        lon_padded = extended(col_edges, (("lon", 2),), 1, True)
        lat_padded = extended(row_edges, (("lat", 1),), 1, False)
        mirror = row_edges[:, 1, :]
        for bit_index in range(bit_total):
            mirror = from_partner(mirror, "lon", bit_index)
        fold_row = sign_rows * mirror[:, ::-1]
        west_edge = lon_padded[:, :, 0]
        east_edge = lon_padded[:, :, 3]
        south_edge = lat_padded[:, 0, :]
        north_edge = jnp.where(is_top, fold_row, lat_padded[:, 3, :])
        east_rows = neighbour(field_rows, east_edge[:-1], 2, -1, last_col)
        west_rows = neighbour(field_rows, west_edge[:-1], 2, 1, first_col)
        north_rows = neighbour(field_rows, north_edge[:-1], 1, -1, last_row)
        south_rows = neighbour(field_rows, south_edge[:-1], 1, 1, first_row)
        wet_east = neighbour(wet_mask, east_edge[-1], 1, -1, last_col)
        wet_west = neighbour(wet_mask, west_edge[-1], 1, 1, first_col)
        wet_north = neighbour(wet_mask, north_edge[-1], 0, -1, last_row)
        wet_south = neighbour(wet_mask, south_edge[-1], 0, 1, first_row)
        shape_four = (4, levels, rows_local, cols_local)
        fields = field_rows.reshape(shape_four)
        fields_east = east_rows.reshape(shape_four)
        fields_west = west_rows.reshape(shape_four)
        fields_north = north_rows.reshape(shape_four)
        fields_south = south_rows.reshape(shape_four)
        laplace = wet_east * (fields_east - fields) + wet_west * (fields_west - fields)
        laplace = (
            laplace + wet_north * (fields_north - fields) + wet_south * (fields_south - fields)
        )
        zonal_vel = fields[2]
        merid_vel = fields[3]
        advect = 0.5 * (
            zonal_vel * (fields_east - fields_west) + merid_vel * (fields_north - fields_south)
        )
        level_above = level_shift(fields, 1, top_level)
        level_below = level_shift(fields, -1, bottom_level)
        vertical = level_above + level_below - 2.0 * fields
        grad_east = 0.5 * (pressure(fields_east) - pressure(fields_west))
        grad_north = 0.5 * (pressure(fields_north) - pressure(fields_south))
        tend_temp = -advect[0] + mixing * laplace[0] + VERTICAL_MIX * vertical[0]
        tend_salt = -advect[1] + mixing * laplace[1] + VERTICAL_MIX * vertical[1]
        tend_zonal = (
            -advect[2]
            + coriolis * merid_vel
            - grad_east
            + VISCOSITY * laplace[2]
            + VERTICAL_MIX * vertical[2]
        )
        tend_merid = (
            -advect[3]
            - coriolis * zonal_vel
            - grad_north
            + VISCOSITY * laplace[3]
            + VERTICAL_MIX * vertical[3]
        )
        tendency = jnp.stack([tend_temp, tend_salt, tend_zonal, tend_merid])
        updated = wet_mask * (fields + TIMESTEP * tendency)
        field_rows = updated.reshape(4 * levels, rows_local, cols_local)
    fields = field_rows.reshape(4, levels, rows_local, cols_local)
    surface = jnp.concatenate([fields[:, 0], wet_mask[None]], axis=0)
    blocks = (
        surface.reshape(5, rows_local, cols_local // 128, 128)
        .transpose(1, 2, 0, 3)
        .reshape(-1, 5, 128)
    )
    block_count = blocks.shape[0]
    devices = lon_count * lat_count
    capacity = max(2, 2 * block_count // devices)
    owner_ids = owners[:, 0]
    onehot = (owner_ids[:, None] == jnp.arange(devices, dtype=jnp.int32)[None, :]).astype(jnp.int32)
    position = jnp.sum((jnp.cumsum(onehot, axis=0) - 1) * onehot, axis=1)
    slot_index = owner_ids * capacity + position
    outgoing = jnp.zeros((devices * capacity, 5, 128), jnp.float32).at[slot_index].set(blocks)
    outgoing_rows = jnp.full((devices * capacity,), -1, jnp.int32).at[slot_index].set(atm_row)
    sectioned_blocks = outgoing.reshape(lon_count, lat_count, capacity, 5, 128)
    sectioned_rows = outgoing_rows.reshape(lon_count, lat_count, capacity)
    sectioned_blocks, sectioned_rows = (
        exchange_both(sectioned_blocks, ("lon", "lat"), ("lon", "lat"), (0, 1), (0, 1)),
        exchange_both(sectioned_rows, ("lon", "lat"), ("lon", "lat"), (0, 1), (0, 1)),
    )
    incoming = sectioned_blocks.reshape(devices * capacity, 5, 128)
    incoming_rows = sectioned_rows.reshape(devices * capacity)
    row_onehot = (incoming_rows[:, None] == jnp.arange(ATM_ROWS, dtype=jnp.int32)[None, :]).astype(
        jnp.float32
    )
    totals = lax.dot_general(
        row_onehot,
        incoming.reshape(devices * capacity, 640),
        (((0,), (0,)), ((), ())),
        precision=lax.Precision.HIGHEST,
        preferred_element_type=jnp.float32,
    )
    totals = totals.reshape(ATM_ROWS, 5, 128)
    ocean_count = totals[:, 4]
    atm_surface = (totals[:, :4] / jnp.maximum(ocean_count, 1.0)[:, None]).transpose(1, 0, 2)
    return (fields[:2], fields[2:], atm_surface, ocean_count)


def solution(mesh):
    in_specs = (
        P(None, None, "lat", "lon"),
        P(None, None, "lat", "lon"),
        P("lat", "lon"),
        P("lat", "lon"),
        P(("lon", "lat"), None),
        P(("lon", "lat")),
    )
    out_specs = (
        P(None, None, "lat", "lon"),
        P(None, None, "lat", "lon"),
        P(None, ("lon", "lat"), None),
        P(("lon", "lat"), None),
    )
    return jax.shard_map(local, mesh=mesh, in_specs=in_specs, out_specs=out_specs, check_vma=False)
```

profile of v0, /device:TPU:1, one launch (start us, length us, event | category | flops | bytes accessed | tf_op | source)
XLA Modules:
  0.0 216.1 jit_solution(3611816705176041696)
XLA Ops:
  0.6 1.3 convert_bitcast_fusion
  2.0 1.8 copy_multiply_fusion
  8.6 6.6 %collective-permute-start = (f32[65,32,1]{0,1,2:T(8,128)}, f32[65,32,1]{0,1,2:T(8,128)}, u32[]{:S(2)}, u32[]{:S(2)}) collective-permute-start(f32[65,32,1]{0,1,2:T(8,128)} %get-tuple-element.69), channel_id=1, source_target_pairs={{16,0},{32,16},{48,32},{64,48},{80,64},{96,80},{112,96},{0,112},{1... | collective-permute-start | bytes 24968 | tf_op jit(solution)/shard_map/ppermute | solution.py:29
  17.0 2.9 %collective-permute-start.5 = (f32[65,1,128]{2,0,1:T(8,128)}, f32[65,1,128]{2,0,1:T(8,128)}, u32[]{:S(2)}, u32[]{:S(2)}) collective-permute-start(f32[65,1,128]{2,0,1:T(8,128)} %get-tuple-element.57), channel_id=1, source_target_pairs={{1,0},{2,1},{3,2},{4,3},{5,4},{6,5},{7,6},{8,7},{9,8},{10,9},{11,1... | collective-permute-start | bytes 99848 | tf_op jit(solution)/shard_map/ppermute | solution.py:29
  19.9 3.1 %collective-permute-start.6 = (f32[65,1,128]{2,0,1:T(8,128)}, f32[65,1,128]{2,0,1:T(8,128)}, u32[]{:S(2)}, u32[]{:S(2)}) collective-permute-start(f32[65,1,128]{2,0,1:T(8,128)} %get-tuple-element.58), channel_id=1, source_target_pairs={{0,1},{1,2},{2,3},{3,4},{4,5},{5,6},{6,7},{7,8},{8,9},{9,10},{10,1... | collective-permute-start | bytes 99848 | tf_op jit(solution)/shard_map/ppermute | solution.py:28
  24.9 12.1 %all-to-all-start = ((s32[128,1,1,2]{3,2,1,0:T(1,128)}), s32[128,1,1,2]{3,2,1,0:T(1,128)}, u32[]{:S(2)}, u32[]{:S(2)}) async-start(s32[128,1,1,2]{3,2,1,0:T(1,128)} %bitcast.69), calls=%async_computation | async-start | bytes 131072 | tf_op jit(solution)/shard_map/all_to_all | solution.py:56
  38.4 1.6 fusion.102
  42.1 1.6 fusion.104
  44.3 2.0 fusion.12
  46.2 1.0 copy-done.17
  47.9 2.4 %copy.259 = f32[64,32,1]{1,0,2:T(8,128)} copy(f32[64,32,1]{2,0,1:T(8,128)} %copy-done.4) | data formatting | bytes 16384 | tf_op jit(solution)/shard_map/slice | solution.py:117
  50.3 2.4 %copy.264 = f32[64,32,1]{1,0,2:T(8,128)} copy(f32[64,32,1]{2,0,1:T(8,128)} %copy-done.5) | data formatting | bytes 16384 | tf_op jit(solution)/shard_map/slice | solution.py:117
  52.6 1.6 copy.251
  54.2 2.2 %copy.261 = f32[4,16,32,1]{3,1,2,0:T(8,128)} copy(f32[4,16,32,1]{2,1,0,3:T(8,128)} %bitcast.213) | data formatting | bytes 16384 | tf_op jit(solution)/shard_map/jit(_roll_static)/concatenate | solution.py:71
  56.4 2.2 %copy.265 = f32[4,16,32,1]{3,1,2,0:T(8,128)} copy(f32[4,16,32,1]{2,1,0,3:T(8,128)} %bitcast.212) | data formatting | bytes 16384 | tf_op jit(solution)/shard_map/jit(_roll_static)/concatenate | solution.py:71
  58.6 1.3 slice_bitcast_fusion.13
  60.0 1.3 slice_bitcast_fusion.12
  61.9 2.5 %maximum_select_fusion.6 = (f32[64,32,128]{2,0,1:T(8,128)S(1)}, f32[64,32,128]{2,0,1:T(8,128)S(1)}) fusion(f32[64,32,1]{2,0,1:T(8,128)} %copy-done.4, f32[64,32,127]{2,0,1:T(8,128)S(1)} %get-tuple-element.40, f32[64,32]{0,1:T(8,128)S(1)} %get-tuple-element.77, pred[128]{0:T(512)(128)(4,1)S(1)} %copy-done.75, f32[64,32,127]{2,0,1:T(8,128)S(1)} %get-tuple-element.41, ...), kind=kLoop, calls=%fused_computation.24 | loop fusion | flops 1048576 | bytes 4210944 | tf_op jit(solution)/shard_map/jit(_where)/select_n | solution.py:72
  64.5 0.9 fusion.63
  71.0 1.4 copy.404
  72.4 1.5 copy.263
  73.9 1.4 slice_bitcast_fusion.15
  75.9 1.3 maximum_select_fusion.9
  77.2 1.0 copy-done.19
  79.1 2.9 %collective-permute-start.3 = (f32[65,128]{1,0:T(8,128)}, f32[65,128]{1,0:T(8,128)S(1)}, u32[]{:S(2)}, u32[]{:S(2)}) collective-permute-start(f32[65,128]{1,0:T(8,128)} %collective-permute-done.2), channel_id=1, source_target_pairs={{0,32},{16,48},{32,0},{48,16},{64,96},{80,112},{96,64},{112,80},{1... | collective-permute-start | bytes 99848 | tf_op jit(solution)/shard_map/ppermute | solution.py:35
  82.6 1.0 collective-permute-done.3
  83.6 3.3 %collective-permute-start.4 = (f32[65,128]{1,0:T(8,128)S(1)}, f32[65,128]{1,0:T(8,128)}, u32[]{:S(2)}, u32[]{:S(2)}) collective-permute-start(f32[65,128]{1,0:T(8,128)S(1)} %collective-permute-done.3), channel_id=1, source_target_pairs={{0,64},{16,80},{32,96},{48,112},{64,0},{80,16},{96,32},{112,48},{1... | collective-permute-start | bytes 99848 | tf_op jit(solution)/shard_map/ppermute | solution.py:35
  88.3 1.5 rev.6
  89.8 0.9 bitcast_select_fusion.1
  90.7 1.5 maximum_select_fusion.8
  94.3 2.6 %add_multiply_fusion.2 = f32[4,16,32,128]{3,1,2,0:T(8,128)S(1)} fusion(f32[4,16,1,128]{3,1,2,0:T(8,128)S(1)} %bitcast.195, f32[4,16,1,128]{3,1,2,0:T(8,128)S(1)} %bitcast.193, f32[4,16,128]{2,1,0:T(8,128)} %bitcast.210, f32[4,16,128]{2,1,0:T(8,128)S(1)} %bitcast.206, f32[16,32,128]{2,0,1:T(8,128)S(1)} %copy-done.34, f32[16,32,128]{2,0,1:T(8,128)S(1)} %copy-done.33, ...), kind=kLoop, calls=%fused_computation.50 | loop fusion | flops 3670016 | bytes 5849408 | tf_op jit(solution)/shard_map/mul | solution.py:159
  97.0 1.5 multiply_add_fusion.1
  102.0 1.7 fusion.95
  103.8 1.3 fusion.94
  105.1 1.6 fusion.96
  108.1 1.5 fusion.97
  109.8 1.6 copy.323
  111.3 1.6 copy.324
  113.1 5.2 %collective-permute-start.7 = (f32[65,32,1]{0,1,2:T(8,128)S(1)}, f32[65,32,1]{0,1,2:T(8,128)S(1)}, u32[]{:S(2)}, u32[]{:S(2)}) collective-permute-start(f32[65,32,1]{0,1,2:T(8,128)S(1)} %get-tuple-element.67), channel_id=1, source_target_pairs={{16,0},{32,16},{48,32},{64,48},{80,64},{96,80},{112,96},{0,112},{1... | collective-permute-start | bytes 24968 | tf_op jit(solution)/shard_map/ppermute | solution.py:29
  120.3 6.0 %collective-permute-start.13 = (f32[65,1,128]{2,0,1:T(8,128)}, f32[65,1,128]{2,0,1:T(8,128)}, u32[]{:S(2)}, u32[]{:S(2)}) collective-permute-start(f32[65,1,128]{2,0,1:T(8,128)} %copy.548), channel_id=1, source_target_pairs={{0,1},{1,2},{2,3},{3,4},{4,5},{5,6},{6,7},{7,8},{8,9},{9,10},{10,1... | collective-permute-start | bytes 99848 | tf_op jit(solution)/shard_map/ppermute | solution.py:28
  126.4 2.1 collective-permute-start.12
  129.1 3.4 %fusion.14 = f32[4,16,32,128]{3,1,2,0:T(8,128)} fusion(f32[4,15,32,128]{3,1,2,0:T(8,128)} %get-tuple-element.32, f32[4,1,32,128]{3,1,2,0:T(1,128)S(1)} %get-tuple-element.34, f32[4,1,32,128]{3,1,2,0:T(1,128)S(1)} %get-tuple-element.33, f32[4,15,32,128]{3,1,2,0:T(8,128)} %get-tuple-element.31, pred[16]{0:T(512)(128)(4,1)S(1)} %copy-done.88, ...), kind=kLoop, calls=%fused_computation.35 | loop fusion | flops 1835008 | bytes 4194336 | tf_op jit(solution)/shard_map/sub | solution.py:164
  132.6 1.8 copy.328
  134.3 1.8 copy.333
  136.1 1.4 copy.330
  137.5 1.5 copy.334
  139.0 2.9 %copy.374 = f32[64,31,128]{2,1,0:T(8,128)} copy(f32[64,31,128]{2,0,1:T(8,128)} %get-tuple-element.30) | data formatting | bytes 2031616 | tf_op jit(solution)/shard_map/jit(_roll_static)/slice | solution.py:71
  146.1 0.9 copy-done.25
  152.1 1.4 slice_bitcast_fusion.14
  154.1 1.3 maximum_select_fusion.19
  156.2 3.6 %collective-permute-start.10 = (f32[65,128]{1,0:T(8,128)}, f32[65,128]{1,0:T(8,128)S(1)}, u32[]{:S(2)}, u32[]{:S(2)}) collective-permute-start(f32[65,128]{1,0:T(8,128)} %collective-permute-done.9), channel_id=1, source_target_pairs={{0,32},{16,48},{32,0},{48,16},{64,96},{80,112},{96,64},{112,80},{1... | collective-permute-start | bytes 99848 | tf_op jit(solution)/shard_map/ppermute | solution.py:35
  161.4 3.2 %collective-permute-start.11 = (f32[65,128]{1,0:T(8,128)S(1)}, f32[65,128]{1,0:T(8,128)}, u32[]{:S(2)}, u32[]{:S(2)}) collective-permute-start(f32[65,128]{1,0:T(8,128)S(1)} %collective-permute-done.10), channel_id=1, source_target_pairs={{0,64},{16,80},{32,96},{48,112},{64,0},{80,16},{96,32},{112,48},{1... | collective-permute-start | bytes 99848 | tf_op jit(solution)/shard_map/ppermute | solution.py:35
  166.0 1.5 rev.7
  167.5 0.9 bitcast_select_fusion
  169.2 1.6 maximum_select_fusion.18
  171.0 1.1 copy-done.1
  172.2 2.8 %add_multiply_fusion = f32[4,16,32,128]{3,1,2,0:T(8,128)S(1)} fusion(f32[4,16,1,128]{3,1,2,0:T(8,128)S(1)} %bitcast.198, f32[4,16,1,128]{3,1,2,0:T(8,128)S(1)} %bitcast.202, f32[4,16,128]{2,1,0:T(8,128)S(1)} %bitcast.208, f32[4,16,128]{2,1,0:T(8,128)S(1)} %bitcast.204, f32[16,32,128]{2,0,1:T(8,128)S(1)} %copy-done.32, f32[16,32,128]{2,0,1:T(8,128)S(1)} %copy-done.31, ...), kind=kLoop, calls=%fused_computation.47 | loop fusion | flops 3670016 | bytes 5849408 | tf_op jit(solution)/shard_map/mul | solution.py:159
  175.2 3.5 %multiply_add_fusion = f32[4,16,32,128]{3,1,2,0:T(8,128)S(1)} fusion(f32[4,16,1,128]{3,1,2,0:T(8,128)S(1)} %bitcast.199, f32[4,16,1,128]{3,1,2,0:T(8,128)S(1)} %bitcast.203, f32[32,128]{1,0:T(8,128)S(1)} %copy-done.60, f32[32,128]{1,0:T(8,128)S(1)} %fusion.81, f32[32,128]{1,0:T(8,128)S(1)} %copy-done.57, f32[32,128]{1,0:T(8,128)S(1)} %copy-done.56, ...), kind=kLoop, calls=%fused_computation.46 | loop fusion | flops 4980736 | bytes 6439232 | tf_op jit(solution)/shard_map/add | solution.py:155
  183.6 1.5 scatter_fusion
  185.0 1.2 copy.386
  186.2 12.2 %all-to-all-start.1 = ((f32[128,1,1,2,5,128]{5,3,4,2,1,0:T(2,128)}), f32[128,1,1,2,5,128]{5,3,4,2,1,0:T(2,128)S(1)}, u32[]{:S(2)}, u32[]{:S(2)}) async-start(f32[128,1,1,2,5,128]{5,3,4,2,1,0:T(2,128)} %copy.386), calls=%async_computation.1 | async-start | bytes 1310720 | tf_op jit(solution)/shard_map/all_to_all | solution.py:56
  198.5 1.0 eq.159
  199.5 1.0 fusion.92
  200.5 13.4 %all-to-all-done.1 = f32[128,1,1,2,5,128]{5,3,4,2,1,0:T(2,128)S(1)} async-done(((f32[128,1,1,2,5,128]{5,3,4,2,1,0:T(2,128)}), f32[128,1,1,2,5,128]{5,3,4,2,1,0:T(2,128)S(1)}, u32[]{:S(2)}, u32[]{:S(2)}) %all-to-all-start.1) | async-done | bytes 655392 | tf_op jit(solution)/shard_map/all_to_all | solution.py:56
  (313 shorter events, 54.2 us)
Async XLA Ops:
  2.0 65.1 %copy-start.46 = (f32[32,1]{1,0:T(8,128)}, f32[32,1]{1,0:T(8,128)S(1)}, u32[]{:S(2)}) copy-start(f32[32,1]{1,0:T(8,128)S(1)} %get-tuple-element.83) | copy-start | bytes 388
  2.0 66.7 %copy-start.44 = (f32[32,1]{1,0:T(8,128)}, f32[32,1]{1,0:T(8,128)S(1)}, u32[]{:S(2)}) copy-start(f32[32,1]{1,0:T(8,128)S(1)} %get-tuple-element.84) | copy-start | bytes 388
  8.6 50.0 %collective-permute-start = (f32[65,32,1]{0,1,2:T(8,128)}, f32[65,32,1]{0,1,2:T(8,128)}, u32[]{:S(2)}, u32[]{:S(2)}) collective-permute-start(f32[65,32,1]{0,1,2:T(8,128)} %get-tuple-element.69), channel_id=1, source_target_pairs={{16,0},{32,16},{48,32},{64,48},{80,64},{96,80},{112,96},{0,112},{1... | collective-permute-start | bytes 24968 | tf_op jit(solution)/shard_map/ppermute | solution.py:29
  15.2 44.7 %collective-permute-start.1 = (f32[65,32,1]{0,1,2:T(8,128)}, f32[65,32,1]{0,1,2:T(8,128)}, u32[]{:S(2)}, u32[]{:S(2)}) collective-permute-start(f32[65,32,1]{0,1,2:T(8,128)} %get-tuple-element.70), channel_id=1, source_target_pairs={{0,16},{16,32},{32,48},{48,64},{64,80},{80,96},{96,112},{112,0},{1... | collective-permute-start | bytes 24968 | tf_op jit(solution)/shard_map/ppermute | solution.py:28
  17.0 62.1 %collective-permute-start.2 = (f32[65,128]{1,0:T(8,128)}, f32[65,128]{1,0:T(8,128)}, u32[]{:S(2)}, u32[]{:S(2)}) collective-permute-start(f32[65,128]{1,0:T(8,128)} %get-tuple-element.56), channel_id=1, source_target_pairs={{0,16},{16,0},{32,48},{48,32},{64,80},{80,64},{96,112},{112,96},{1... | collective-permute-start | bytes 99848 | tf_op jit(solution)/shard_map/ppermute | solution.py:35
  17.0 72.7 %collective-permute-start.5 = (f32[65,1,128]{2,0,1:T(8,128)}, f32[65,1,128]{2,0,1:T(8,128)}, u32[]{:S(2)}, u32[]{:S(2)}) collective-permute-start(f32[65,1,128]{2,0,1:T(8,128)} %get-tuple-element.57), channel_id=1, source_target_pairs={{1,0},{2,1},{3,2},{4,3},{5,4},{6,5},{7,6},{8,7},{9,8},{10,9},{11,1... | collective-permute-start | bytes 99848 | tf_op jit(solution)/shard_map/ppermute | solution.py:29
  19.9 3.1 %copy-start.91 = (s32[32,1]{0,1:T(1,128)S(1)}, s32[32,1]{0,1:T(1,128)}, u32[]{:S(2)}) copy-start(s32[32,1]{0,1:T(1,128)} %param.10) | copy-start | bytes 388
  19.9 54.0 %collective-permute-start.6 = (f32[65,1,128]{2,0,1:T(8,128)}, f32[65,1,128]{2,0,1:T(8,128)}, u32[]{:S(2)}, u32[]{:S(2)}) collective-permute-start(f32[65,1,128]{2,0,1:T(8,128)} %get-tuple-element.58), channel_id=1, source_target_pairs={{0,1},{1,2},{2,3},{3,4},{4,5},{5,6},{6,7},{7,8},{8,9},{9,10},{10,1... | collective-permute-start | bytes 99848 | tf_op jit(solution)/shard_map/ppermute | solution.py:28
  24.9 161.3 %all-to-all-start = ((s32[128,1,1,2]{3,2,1,0:T(1,128)}), s32[128,1,1,2]{3,2,1,0:T(1,128)}, u32[]{:S(2)}, u32[]{:S(2)}) async-start(s32[128,1,1,2]{3,2,1,0:T(1,128)} %bitcast.69), calls=%async_computation | async-start | bytes 131072 | tf_op jit(solution)/shard_map/all_to_all | solution.py:56
  38.4 1.6 copy-start.15
  42.1 25.1 %copy-start.50 = (f32[32,127]{1,0:T(8,128)}, f32[32,127]{1,0:T(8,128)S(1)}, u32[]{:S(2)}) copy-start(f32[32,127]{1,0:T(8,128)S(1)} %get-tuple-element.81) | copy-start | bytes 48772
  42.1 26.7 %copy-start.48 = (f32[32,127]{1,0:T(8,128)}, f32[32,127]{1,0:T(8,128)S(1)}, u32[]{:S(2)}) copy-start(f32[32,127]{1,0:T(8,128)S(1)} %get-tuple-element.82) | copy-start | bytes 48772
  78.3 8.6 %copy-start.52 = (f32[31,128]{1,0:T(8,128)S(1)}, f32[31,128]{1,0:T(8,128)}, u32[]{:S(2)}) copy-start(f32[31,128]{1,0:T(8,128)} %get-tuple-element.86) | copy-start | bytes 47620
  79.1 4.5 %collective-permute-start.3 = (f32[65,128]{1,0:T(8,128)}, f32[65,128]{1,0:T(8,128)S(1)}, u32[]{:S(2)}, u32[]{:S(2)}) collective-permute-start(f32[65,128]{1,0:T(8,128)} %collective-permute-done.2), channel_id=1, source_target_pairs={{0,32},{16,48},{32,0},{48,16},{64,96},{80,112},{96,64},{112,80},{1... | collective-permute-start | bytes 99848 | tf_op jit(solution)/shard_map/ppermute | solution.py:35
  82.6 4.3 %copy-start.82 = (f32[1,128]{1,0:T(1,128)S(1)}, f32[1,128]{1,0:T(1,128)}, u32[]{:S(2)}) copy-start(f32[1,128]{1,0:T(1,128)} %copy-done.81) | copy-start | bytes 1540
  83.6 4.7 %collective-permute-start.4 = (f32[65,128]{1,0:T(8,128)S(1)}, f32[65,128]{1,0:T(8,128)}, u32[]{:S(2)}, u32[]{:S(2)}) collective-permute-start(f32[65,128]{1,0:T(8,128)S(1)} %collective-permute-done.3), channel_id=1, source_target_pairs={{0,64},{16,80},{32,96},{48,112},{64,0},{80,16},{96,32},{112,48},{1... | collective-permute-start | bytes 99848 | tf_op jit(solution)/shard_map/ppermute | solution.py:35
  89.8 3.9 %copy-start.34 = (f32[16,32,128]{2,0,1:T(8,128)S(1)}, f32[16,32,128]{2,0,1:T(8,128)}, u32[]{:S(2)}) copy-start(f32[16,32,128]{2,0,1:T(8,128)} %get-tuple-element.53) | copy-start | bytes 786436
  90.7 3.0 %copy-start.8 = (f32[64,31,128]{2,0,1:T(8,128)S(1)}, f32[64,31,128]{2,0,1:T(8,128)}, u32[]{:S(2)}) copy-start(f32[64,31,128]{2,0,1:T(8,128)} %get-tuple-element.45) | copy-start | bytes 3047428
  90.7 3.0 %copy-start.12 = (f32[4,16,32,1]{3,1,2,0:T(8,128)S(1)}, f32[4,16,32,1]{3,1,2,0:T(8,128)}, u32[]{:S(2)}) copy-start(f32[4,16,32,1]{3,1,2,0:T(8,128)} %copy.261) | copy-start | bytes 24580
  94.2 2.6 %copy-start.13 = (f32[4,16,32,1]{3,1,2,0:T(8,128)S(1)}, f32[4,16,32,1]{3,1,2,0:T(8,128)}, u32[]{:S(2)}) copy-start(f32[4,16,32,1]{3,1,2,0:T(8,128)} %copy.265) | copy-start | bytes 24580
  94.2 2.6 %copy-start.41 = (f32[64,1,128]{2,0,1:T(8,128)S(1)}, f32[64,1,128]{2,0,1:T(8,128)}, u32[]{:S(2)}) copy-start(f32[64,1,128]{2,0,1:T(8,128)} %get-tuple-element.64) | copy-start | bytes 98308
  94.2 2.7 %copy-start.58 = (f32[32,128]{1,0:T(8,128)S(1)}, f32[32,128]{1,0:T(8,128)}, u32[]{:S(2)}) copy-start(f32[32,128]{1,0:T(8,128)} %broadcast_select_fusion.3) | copy-start | bytes 49156
  94.2 2.7 %copy-start.59 = (f32[32,128]{1,0:T(8,128)S(1)}, f32[32,128]{1,0:T(8,128)}, u32[]{:S(2)}) copy-start(f32[32,128]{1,0:T(8,128)} %broadcast_select_fusion.2) | copy-start | bytes 49156
  94.3 2.7 %copy-start.61 = (f32[32,128]{1,0:T(8,128)S(1)}, f32[32,128]{1,0:T(8,128)}, u32[]{:S(2)}) copy-start(f32[32,128]{1,0:T(8,128)} %fusion.80) | copy-start | bytes 49156
  96.9 1.6 copy-start.16
  96.9 1.6 copy-start.18
  96.9 1.7 copy-start.20
  97.0 1.7 copy-start.30
  97.0 1.7 copy-start.54
  97.0 1.7 copy-start.85
  111.3 1.6 copy-start.43
  113.1 28.9 %collective-permute-start.7 = (f32[65,32,1]{0,1,2:T(8,128)S(1)}, f32[65,32,1]{0,1,2:T(8,128)S(1)}, u32[]{:S(2)}, u32[]{:S(2)}) collective-permute-start(f32[65,32,1]{0,1,2:T(8,128)S(1)} %get-tuple-element.67), channel_id=1, source_target_pairs={{16,0},{32,16},{48,32},{64,48},{80,64},{96,80},{112,96},{0,112},{1... | collective-permute-start | bytes 24968 | tf_op jit(solution)/shard_map/ppermute | solution.py:29
  118.3 25.8 %collective-permute-start.8 = (f32[65,32,1]{0,1,2:T(8,128)S(1)}, f32[65,32,1]{0,1,2:T(8,128)S(1)}, u32[]{:S(2)}, u32[]{:S(2)}) collective-permute-start(f32[65,32,1]{0,1,2:T(8,128)S(1)} %get-tuple-element.68), channel_id=1, source_target_pairs={{0,16},{16,32},{32,48},{48,64},{64,80},{80,96},{96,112},{112,0},{1... | collective-permute-start | bytes 24968 | tf_op jit(solution)/shard_map/ppermute | solution.py:28
  120.3 31.9 %collective-permute-start.13 = (f32[65,1,128]{2,0,1:T(8,128)}, f32[65,1,128]{2,0,1:T(8,128)}, u32[]{:S(2)}, u32[]{:S(2)}) collective-permute-start(f32[65,1,128]{2,0,1:T(8,128)} %copy.548), channel_id=1, source_target_pairs={{0,1},{1,2},{2,3},{3,4},{4,5},{5,6},{6,7},{7,8},{8,9},{9,10},{10,1... | collective-permute-start | bytes 99848 | tf_op jit(solution)/shard_map/ppermute | solution.py:28
  126.3 29.9 %collective-permute-start.9 = (f32[65,128]{1,0:T(8,128)}, f32[65,128]{1,0:T(8,128)}, u32[]{:S(2)}, u32[]{:S(2)}) collective-permute-start(f32[65,128]{1,0:T(8,128)} %bitcast.150.clone.2), channel_id=1, source_target_pairs={{0,16},{16,0},{32,48},{48,32},{64,80},{80,64},{96,112},{112,96},{1... | collective-permute-start | bytes 99848 | tf_op jit(solution)/shard_map/ppermute | solution.py:35
  126.4 41.1 %collective-permute-start.12 = (f32[65,1,128]{2,1,0:T(1,128)}, f32[65,1,128]{2,1,0:T(1,128)}, u32[]{:S(2)}, u32[]{:S(2)}) collective-permute-start(f32[65,1,128]{2,1,0:T(1,128)} %get-tuple-element.60), channel_id=1, source_target_pairs={{1,0},{2,1},{3,2},{4,3},{5,4},{6,5},{7,6},{8,7},{9,8},{10,9},{11,1... | collective-permute-start | bytes 99848 | tf_op jit(solution)/shard_map/ppermute | solution.py:29
  139.0 3.0 %copy-start.3 = (f32[64,32,1]{2,0,1:T(8,128)S(1)}, f32[64,32,1]{2,0,1:T(8,128)}, u32[]{:S(2)}) copy-start(f32[64,32,1]{2,0,1:T(8,128)} %get-tuple-element.27) | copy-start | bytes 24580
  142.6 2.1 copy-start.2
  143.2 2.8 %copy-start.23 = (f32[64,32,128]{2,0,1:T(8,128)}, f32[64,32,128]{2,0,1:T(8,128)S(1)}, u32[]{:S(2)}) copy-start(f32[64,32,128]{2,0,1:T(8,128)S(1)} %maximum_select_fusion.16) | copy-start | bytes 3145732
  143.2 1.8 copy-start
  146.0 1.9 copy-start.51
  146.0 3.3 %copy-start.49 = (f32[32,127]{1,0:T(8,128)S(1)}, f32[32,127]{1,0:T(8,128)}, u32[]{:S(2)}) copy-start(f32[32,127]{1,0:T(8,128)} %copy-done.48) | copy-start | bytes 48772
  155.5 9.1 %copy-start.53 = (f32[31,128]{1,0:T(8,128)S(1)}, f32[31,128]{1,0:T(8,128)}, u32[]{:S(2)}) copy-start(f32[31,128]{1,0:T(8,128)} %get-tuple-element.86) | copy-start | bytes 47620
  156.2 8.4 %copy-start.83 = (f32[1,128]{1,0:T(1,128)S(1)}, f32[1,128]{1,0:T(1,128)}, u32[]{:S(2)}) copy-start(f32[1,128]{1,0:T(1,128)} %copy-done.81) | copy-start | bytes 1540
  156.2 5.2 %collective-permute-start.10 = (f32[65,128]{1,0:T(8,128)}, f32[65,128]{1,0:T(8,128)S(1)}, u32[]{:S(2)}, u32[]{:S(2)}) collective-permute-start(f32[65,128]{1,0:T(8,128)} %collective-permute-done.9), channel_id=1, source_target_pairs={{0,32},{16,48},{32,0},{48,16},{64,96},{80,112},{96,64},{112,80},{1... | collective-permute-start | bytes 99848 | tf_op jit(solution)/shard_map/ppermute | solution.py:35
  161.4 4.6 %collective-permute-start.11 = (f32[65,128]{1,0:T(8,128)S(1)}, f32[65,128]{1,0:T(8,128)}, u32[]{:S(2)}, u32[]{:S(2)}) collective-permute-start(f32[65,128]{1,0:T(8,128)S(1)} %collective-permute-done.10), channel_id=1, source_target_pairs={{0,64},{16,80},{32,96},{48,112},{64,0},{80,16},{96,32},{112,48},{1... | collective-permute-start | bytes 99848 | tf_op jit(solution)/shard_map/ppermute | solution.py:35
  167.5 3.5 %copy-start.32 = (f32[16,32,128]{2,0,1:T(8,128)S(1)}, f32[16,32,128]{2,0,1:T(8,128)}, u32[]{:S(2)}) copy-start(f32[16,32,128]{2,0,1:T(8,128)} %get-tuple-element.24) | copy-start | bytes 786436
  169.2 1.8 copy-start.6
  169.2 1.8 copy-start.9
  169.2 1.8 copy-start.38
  169.2 1.8 copy-start.40
  172.2 2.9 %copy-start.10 = (f32[4,16,32,1]{3,1,2,0:T(8,128)S(1)}, f32[4,16,32,1]{3,1,2,0:T(8,128)}, u32[]{:S(2)}) copy-start(f32[4,16,32,1]{3,1,2,0:T(8,128)} %copy.330) | copy-start | bytes 24580
  172.2 2.9 %copy-start.11 = (f32[4,16,32,1]{3,1,2,0:T(8,128)S(1)}, f32[4,16,32,1]{3,1,2,0:T(8,128)}, u32[]{:S(2)}) copy-start(f32[4,16,32,1]{3,1,2,0:T(8,128)} %copy.334) | copy-start | bytes 24580
  172.2 2.9 %copy-start.56 = (f32[32,128]{1,0:T(8,128)S(1)}, f32[32,128]{1,0:T(8,128)}, u32[]{:S(2)}) copy-start(f32[32,128]{1,0:T(8,128)} %broadcast_select_fusion.1) | copy-start | bytes 49156
  172.2 2.9 %copy-start.57 = (f32[32,128]{1,0:T(8,128)S(1)}, f32[32,128]{1,0:T(8,128)}, u32[]{:S(2)}) copy-start(f32[32,128]{1,0:T(8,128)} %broadcast_select_fusion) | copy-start | bytes 49156
  172.2 2.9 %copy-start.60 = (f32[32,128]{1,0:T(8,128)S(1)}, f32[32,128]{1,0:T(8,128)}, u32[]{:S(2)}) copy-start(f32[32,128]{1,0:T(8,128)} %fusion.79) | copy-start | bytes 49156
  175.1 3.6 %copy-start.21 = (f32[4,16,32,128]{3,1,2,0:T(8,128)S(1)}, f32[4,16,32,128]{3,1,2,0:T(8,128)}, u32[]{:S(2)}) copy-start(f32[4,16,32,128]{3,1,2,0:T(8,128)} %fusion.14) | copy-start | bytes 3145732
  175.1 3.6 %copy-start.24 = (f32[64,32,128]{2,0,1:T(8,128)S(1)}, f32[64,32,128]{2,0,1:T(8,128)}, u32[]{:S(2)}) copy-start(f32[64,32,128]{2,0,1:T(8,128)} %copy-done.23) | copy-start | bytes 3145732
  175.1 3.6 %copy-start.26 = (f32[64,32,128]{2,0,1:T(8,128)S(1)}, f32[64,32,128]{2,0,1:T(8,128)}, u32[]{:S(2)}) copy-start(f32[64,32,128]{2,0,1:T(8,128)} %copy-done.25) | copy-start | bytes 3145732
  175.1 3.6 %copy-start.28 = (f32[16,32,128]{2,1,0:T(8,128)S(1)}, f32[16,32,128]{2,1,0:T(8,128)}, u32[]{:S(2)}) copy-start(f32[16,32,128]{2,1,0:T(8,128)} %fusion.53) | copy-start | bytes 786436
  175.1 3.6 %copy-start.29 = (f32[16,32,128]{2,1,0:T(8,128)S(1)}, f32[16,32,128]{2,1,0:T(8,128)}, u32[]{:S(2)}) copy-start(f32[16,32,128]{2,1,0:T(8,128)} %fusion.50) | copy-start | bytes 786436
  175.1 3.6 %copy-start.55 = (f32[32,128]{1,0:T(8,128)S(1)}, f32[32,128]{1,0:T(8,128)}, u32[]{:S(2)}) copy-start(f32[32,128]{1,0:T(8,128)} %param.9) | copy-start | bytes 49156
  175.1 3.6 %copy-start.86 = (f32[32]{0:T(128)S(1)}, f32[32]{0:T(128)}, u32[]{:S(2)}) copy-start(f32[32]{0:T(128)} %sine_multiply_fusion) | copy-start | bytes 388
  186.2 27.7 %all-to-all-start.1 = ((f32[128,1,1,2,5,128]{5,3,4,2,1,0:T(2,128)}), f32[128,1,1,2,5,128]{5,3,4,2,1,0:T(2,128)S(1)}, u32[]{:S(2)}, u32[]{:S(2)}) async-start(f32[128,1,1,2,5,128]{5,3,4,2,1,0:T(2,128)} %copy.386), calls=%async_computation.1 | async-start | bytes 1310720 | tf_op jit(solution)/shard_map/all_to_all | solution.py:56
  (47 other events, 40.2 us)
where the time goes:
time: 219 us; the launch traced here: 216 us
  local copies, waits for them, and re-layouts  84.7 us (39%)
  starting transfers between devices  63.3 us (29%)
  other arithmetic  48.9 us (22%)
  waiting for transfers between devices  16.9 us (8%)
    all_to_all x2, starting transfers between devices, exchange_both(): lax.all_to_all(pieces, axis, split_axis=0, concat_axis=0, tiled=True)  24.4 us
    unnamed x195, local copies, waits for them, and re-layouts  20.3 us
    ppermute x4, starting transfers between devices, extended(): after = lax.ppermute(leading, axis, down)  16.8 us
    select_n x15, other arithmetic, neighbour(): return jnp.where(position, jnp.expand_dims(edge_value, axis), rolled)  15.1 us
    all_to_all x2, waiting for transfers between devices, exchange_both(): lax.all_to_all(pieces, axis, split_axis=0, concat_axis=0, tiled=True)  13.4 us
    ppermute x6, starting transfers between devices, from_partner(): lax.ppermute(shard, axis, [(i, i ^ 1 << distance) for i in range(lax.axis...  13 us
    broadcast_in_dim x12, local copies, waits for them, and re-layouts, neighbour(): return jnp.where(position, jnp.expand_dims(edge_value, axis), rolled)  10.4 us
    ppermute x4, starting transfers between devices, extended(): before = lax.ppermute(last, axis, up)  9.11 us
  transfers between devices with their start and end apart: 16, of which 5 were waited for; matrix products, arithmetic and copies ran while one was open for 50% of the time, Pallas kernels for 0%

commit v1 on v0

v1 whole, which is shorter than its diff:
```python
import functools
import math

import jax
import jax.numpy as jnp
from jax import lax
from jax.experimental import pallas as pl
from jax.experimental.pallas import tpu as pltpu
from jax.sharding import PartitionSpec as P

THERMAL = 0.2
HALINE = 0.15
GRAVITY = 0.2
TIMESTEP = 0.8
VERTICAL_MIX = 0.1
VISCOSITY = 0.2
CORIOLIS_MAX = 0.3
ATM_ROWS = 32

MESH = pl.DeviceIdType.MESH
ROW0 = 8
f32 = jnp.float32
bf16 = jnp.bfloat16


def iota(shape, dim):
    return lax.broadcasted_iota(jnp.int32, shape, dim)


def split3(x):
    hi = x.astype(bf16)
    rest = x - hi.astype(f32)
    mid = rest.astype(bf16)
    lo = (rest - mid.astype(f32)).astype(bf16)
    return hi, mid, lo


def dot(a, b):
    return lax.dot_general(a, b, (((1,), (0,)), ((), ())), preferred_element_type=f32)


def reverse_lanes(x):
    lane = iota(x.shape, x.ndim - 1)
    size = x.shape[-1]
    step = size // 2
    while step:
        x = jnp.where(
            (lane & step) == 0,
            pltpu.roll(x, size - step, x.ndim - 1),
            pltpu.roll(x, step, x.ndim - 1),
        )
        step //= 2
    return x


def kernel(
    n_lon, n_lat, levels, rows, cols,
    tracers, velocity, land_mask, mixing, owners, atm_row,
    tracers_out, velocity_out, surface_out, cover_out,
    x0, x1, x2, wet_pad, mask_i, mix_v, own_v, row_v,
    pack0, pack1a, pack1b, from_e0, from_w0, from_ea, from_wa, from_eb, from_wb, wet_e, wet_w,
    edge0, edge2a, edge2b, fold0, fold_wet, fold1,
    coef, onehot, out_early, in_early, out_late, in_late, row_hot, cover_v, surf_v,
    in_sem, out_sem, h_send, h_recv, a_send, a_recv, ready,
):
    devices = n_lon * n_lat
    lon = lax.axis_index("lon")
    lat = lax.axis_index("lat")
    me = lon * n_lat + lat
    top = n_lat - 1
    east = (lax.rem(lon + 1, n_lon), lat)
    west = (lax.rem(lon + n_lon - 1, n_lon), lat)
    north = (lon, lax.min(lat + 1, top))
    south = (lon, lax.max(lat - 1, 0))
    mirror = (n_lon - 1 - lon, lat)
    end = ROW0 + rows
    chunks = rows // 8

    loads = [
        pltpu.make_async_copy(land_mask, mask_i, in_sem.at[0]),
        pltpu.make_async_copy(mixing, mix_v, in_sem.at[1]),
        pltpu.make_async_copy(owners, own_v, in_sem.at[2]),
        pltpu.make_async_copy(atm_row, row_v, in_sem.at[3]),
    ]
    for f in range(4):
        src = (tracers if f < 2 else velocity).at[f % 2]
        loads.append(pltpu.make_async_copy(src, x0.at[:, f, ROW0:end, :], in_sem.at[4 + f]))
    for load in loads:
        load.start()

    barrier = pltpu.get_barrier_semaphore()
    for d in range(1, n_lon):
        pl.semaphore_signal(barrier, inc=1, device_id=(lax.rem(lon + d, n_lon), lat), device_id_type=MESH)
    for d in range(1, n_lat):
        pl.semaphore_signal(barrier, inc=1, device_id=(lon, lax.rem(lat + d, n_lat)), device_id_type=MESH)

    lane8 = iota((8, cols), 1)
    lane = iota((rows, cols), 1)
    first = lane8 == 0
    last = lane8 == cols - 1

    def part(c):
        return slice(ROW0 + 8 * c, ROW0 + 8 * c + 8)

    def packed(tile, value, i):
        where = (lane8 == 2 * i) | (lane8 == lax.rem(2 * i + cols - 1, cols))
        return jnp.where(where, pltpu.roll(value, 2 * i, 1), tile)

    loads[0].wait()
    wet = mask_i[...].astype(f32)
    wet_pad[ROW0:end, :] = wet
    for load in loads[4:]:
        load.wait()

    def prepare(k, tiles):
        tiles = list(tiles)
        for f in range(4):
            for c in range(chunks):
                q = x0[k, f, part(c), :] * wet_pad[part(c), :]
                x0[k, f, part(c), :] = q
                tiles[c] = packed(tiles[c], q, 4 * k + f)
        return tuple(tiles)

    tiles = lax.fori_loop(0, levels, prepare, tuple(jnp.zeros((8, cols), f32) for _ in range(chunks)))
    for c in range(chunks):
        pack0[8 * c : 8 * c + 8, :] = tiles[c]

    @pl.when(lat == 0)
    def _():
        x0[:, :, ROW0 - 1, :] = jnp.zeros((levels, 4, cols), f32)
        x1[:, :, ROW0 - 1, :] = jnp.zeros((levels, 4, cols), f32)
        wet_pad[ROW0 - 1 : ROW0, :] = jnp.zeros((1, cols), f32)

    pl.semaphore_wait(barrier, n_lon + n_lat - 2)

    def remote(src, dst, sem, device):
        return pltpu.make_async_remote_copy(
            src_ref=src, dst_ref=dst, send_sem=h_send.at[sem], recv_sem=h_recv.at[sem],
            device_id=device, device_id_type=MESH,
        )

    def row_copies(x, fold, lo, hi, sem):
        rows_of = lambda ref, r: ref.at[lo:hi, :, r, :]
        up = remote(rows_of(x, end - 1), rows_of(x, ROW0 - 1), sem, north)
        over = remote(rows_of(x, end - 1), fold.at[lo:hi], sem + 1, mirror)
        down = remote(rows_of(x, ROW0), rows_of(x, end), sem + 1, south)
        return up, over, down

    def start_rows(up, over, down):
        pl.when(lat < top)(up.start)
        pl.when(lat == top)(over.start)
        pl.when(lat > 0)(down.start)

    def wait_rows(up, over, down):
        pl.when(lat > 0)(up.wait_recv)
        pl.when(lat == top)(over.wait_recv)
        pl.when(lat < top)(down.wait_recv)

    def drain_rows(up, over, down):
        pl.when(lat < top)(up.wait_send)
        pl.when(lat == top)(over.wait_send)
        pl.when(lat > 0)(down.wait_send)

    def col_copies(pack, from_w, from_e, sem):
        return remote(pack, from_w, sem, east), remote(pack, from_e, sem + 1, west)

    halo0_rows = row_copies(x0, fold0, 0, levels, 0)
    halo0_cols = col_copies(pack0, from_w0, from_e0, 2)
    wet_cols = col_copies(wet_pad.at[ROW0:end, :], wet_w, wet_e, 4)
    one = lambda ref, r: ref.at[r : r + 1, :]
    wet_rows = (
        remote(one(wet_pad, end - 1), one(wet_pad, ROW0 - 1), 6, north),
        remote(one(wet_pad, end - 1), fold_wet, 7, mirror),
        remote(one(wet_pad, ROW0), one(wet_pad, end), 7, south),
    )
    start_rows(*halo0_rows)
    for copy in halo0_cols + wet_cols:
        copy.start()
    start_rows(*wet_rows)

    for d in range(1, n_lat):
        pl.semaphore_signal(ready, inc=1, device_id=(lon, lax.rem(lat + d, n_lat)), device_id_type=MESH)

    loads[2].wait()
    loads[3].wait()
    blocks = rows
    pad_row = lambda ref: jnp.concatenate([ref[...].astype(f32)] * (cols // blocks), axis=1)
    own_lane = pad_row(own_v)
    row_lane = pad_row(row_v)
    sub = iota((blocks, cols), 0)
    own_col = jnp.sum(jnp.where(lane == sub, own_lane, 0.0), axis=1, keepdims=True)
    row_col = jnp.sum(jnp.where(lane == sub, row_lane + 1.0, 0.0), axis=1, keepdims=True)
    same = jnp.where((own_col == own_lane) & (sub < lax.rem(lane, blocks)), 1.0, 0.0)
    position = jnp.sum(same, axis=0, keepdims=True)
    lane1 = iota((1, cols), 1)
    target = own_lane.astype(jnp.int32) * 8 + (lane1 // blocks) * 2 + position.astype(jnp.int32)
    onehot[...] = jnp.where(iota((devices * 8, cols), 0) == target, 1.0, 0.0).astype(bf16)
    early = jnp.concatenate(
        [wet, jnp.broadcast_to(row_col, (blocks, cols)), jnp.zeros((2 * blocks, cols), f32)], axis=0
    )
    out_early[...] = dot(onehot[...], early.astype(bf16)).reshape(devices, 8, cols)
    in_early[pl.ds(me, 1)] = out_early[pl.ds(me, 1)]

    latitude = (lat * rows + iota((rows, cols), 0)).astype(f32)
    coriolis = CORIOLIS_MAX * jnp.sin(math.pi * (-0.43 + 0.93 * (latitude + 0.5) / (n_lat * rows)))
    loads[1].wait()

    for copy in wet_cols:
        copy.wait_recv()
    wait_rows(*wet_rows)

    @pl.when(lat == top)
    def _():
        wet_pad[end : end + 1, :] = reverse_lanes(jnp.broadcast_to(fold_wet[...], (8, cols)))[0:1]

    w_east = pltpu.roll(jnp.where(lane == 0, wet_e[...], wet), cols - 1, 1)
    w_west = pltpu.roll(jnp.where(lane == cols - 1, wet_w[...], wet), 1, 1)
    w_north = wet_pad[ROW0 + 1 : end + 1, :]
    w_south = wet_pad[ROW0 - 1 : end - 1, :]
    total = w_east + w_west + w_north + w_south
    centre = 1.0 - 2.0 * TIMESTEP * VERTICAL_MIX
    for base, rate in ((0, TIMESTEP * mix_v[...]), (5, TIMESTEP * VISCOSITY)):
        coef[base] = wet * (centre - rate * total)
        for j, w in enumerate((w_east, w_west, w_north, w_south)):
            coef[base + 1 + j] = wet * (rate * w)
    coef[10] = (TIMESTEP * VERTICAL_MIX) * wet
    coef[11] = TIMESTEP * coriolis * wet

    pressure_rate = 0.5 * TIMESTEP * GRAVITY
    assert abs(pressure_rate - TIMESTEP * VERTICAL_MIX) < 1e-12

    def level(x, k, edge, carry, store):
        above = lax.max(k - 1, 0) if not isinstance(k, int) else max(k - 1, 0)
        below = lax.min(k + 1, levels - 1) if not isinstance(k, int) else min(k + 1, levels - 1)
        carry = list(carry)
        for c in range(chunks):
            mid, up, down = part(c), slice(ROW0 + 8 * c + 1, ROW0 + 8 * c + 9), slice(ROW0 + 8 * c - 1, ROW0 + 8 * c + 7)
            own = slice(8 * c, 8 * c + 8)
            halo = edge[own, :]
            q, e, w, n, s = [], [], [], [], []
            for f in range(4):
                value = x[k, f, mid, :]
                side = pltpu.roll(halo, lax.rem(2 * cols - 2 * (4 * k + f), cols), 1)
                q.append(value)
                e.append(pltpu.roll(jnp.where(first, side, value), cols - 1, 1))
                w.append(pltpu.roll(jnp.where(last, side, value), 1, 1))
                n.append(x[k, f, up, :])
                s.append(x[k, f, down, :])
            gx = HALINE * (e[1] - w[1]) - THERMAL * (e[0] - w[0])
            gy = HALINE * (n[1] - s[1]) - THERMAL * (n[0] - s[0])
            sx = carry[2 * c] + gx
            sy = carry[2 * c + 1] + gy
            carry[2 * c], carry[2 * c + 1] = sx, sy
            push = (None, None, sx - 0.5 * gx, sy - 0.5 * gy)
            u = (0.5 * TIMESTEP) * q[2]
            v = (0.5 * TIMESTEP) * q[3]
            vert = coef[10, own, :]
            turn = coef[11, own, :]
            for f in range(4):
                if f % 2 == 0:
                    base = 0 if f == 0 else 5
                    a = coef[base, own, :]
                    ce = coef[base + 1, own, :] - u
                    cw = coef[base + 2, own, :] + u
                    cn = coef[base + 3, own, :] - v
                    cs = coef[base + 4, own, :] + v
                column = x[above, f, mid, :] + x[below, f, mid, :]
                if f >= 2:
                    column = column - push[f]
                value = (a * q[f] + vert * column) + (ce * e[f] + cw * w[f]) + (cn * n[f] + cs * s[f])
                if f == 2:
                    value = value + turn * q[3]
                if f == 3:
                    value = value - turn * q[2]
                store(k, f, c, value)
        return tuple(carry)

    def merge(edge, from_e, from_w):
        edge[...] = jnp.where(lax.rem(lane, 2) == 0, from_e[...], from_w[...])

    def unfold(x, fold, lo, hi):
        @pl.when(lat == top)
        def _():
            for k in range(lo, hi, 2):
                width = min(2, hi - k)
                pair = fold[k : k + width].reshape(4 * width, cols)
                pair = reverse_lanes(pair)
                field = lax.rem(iota(pair.shape, 0), 4)
                pair = jnp.where(field < 2, pair, -pair)
                for j in range(width):
                    for f in range(4):
                        x[k + j, f, end : end + 1, :] = pair[4 * j + f : 4 * j + f + 1]

    for copy in halo0_cols:
        copy.wait_recv()
    wait_rows(*halo0_rows)
    merge(edge0, from_e0, from_w0)
    unfold(x0, fold0, 0, levels)

    zeros = tuple(jnp.zeros((8, cols), f32) for _ in range(2 * chunks))
    empty = [jnp.zeros((8, cols), f32) for _ in range(chunks)]

    def step1(k, carry, tiles):
        tiles = list(tiles)

        def store(k, f, c, value):
            x1[k, f, part(c), :] = value
            tiles[c] = packed(tiles[c], value, 4 * k + f)

        carry = level(x0, k, edge0, carry, store)
        return carry, tuple(tiles)

    carry, tiles = step1(0, zeros, empty)
    for c in range(chunks):
        pack1a[8 * c : 8 * c + 8, :] = tiles[c]
    halo1_rows = row_copies(x1, fold1, 0, 1, 8)
    halo1_cols = col_copies(pack1a, from_wa, from_ea, 10)
    start_rows(*halo1_rows)
    for copy in halo1_cols:
        copy.start()

    pl.semaphore_wait(ready, n_lat - 1)

    def exchange(out, into, sem, height):
        def copy(d):
            peer = lax.rem(me + d, devices)
            return pltpu.make_async_remote_copy(
                src_ref=out.at[peer, 0:height, :], dst_ref=into.at[me, 0:height, :],
                send_sem=a_send.at[sem], recv_sem=a_recv.at[sem],
                device_id=(peer // n_lat, lax.rem(peer, n_lat)), device_id_type=MESH,
            )

        def go(d, _):
            copy(d).start()
            return 0

        lax.fori_loop(1, devices, go, 0)
        return pltpu.make_async_remote_copy(
            src_ref=out.at[0 : devices - 1, 0:height, :], dst_ref=into.at[0 : devices - 1, 0:height, :],
            send_sem=a_send.at[sem], recv_sem=a_recv.at[sem],
            device_id=east, device_id_type=MESH,
        )

    early_all = exchange(out_early, in_early, 0, 4)

    carry, tiles = lax.fori_loop(1, levels, lambda k, s: step1(k, *s), (carry, tiles))
    for c in range(chunks):
        pack1b[8 * c : 8 * c + 8, :] = tiles[c]
    halo2_rows = row_copies(x1, fold1, 1, levels, 12)
    halo2_cols = col_copies(pack1b, from_wb, from_eb, 14)
    start_rows(*halo2_rows)
    for copy in halo2_cols:
        copy.start()

    for copy in halo1_cols:
        copy.wait_recv()
    wait_rows(*halo1_rows)
    merge(edge2a, from_ea, from_wa)
    unfold(x1, fold1, 0, 1)

    def store2(k, f, c, value):
        x2[k, f, 8 * c : 8 * c + 8, :] = value

    carry = level(x1, 0, edge2a, zeros, store2)
    surf = x2[0].reshape(4 * rows, cols)
    hot = onehot[...]
    late = sum(dot(hot, piece) for piece in split3(surf))
    out_late[...] = late.reshape(devices, 8, cols)
    in_late[pl.ds(me, 1)] = out_late[pl.ds(me, 1)]
    late_all = exchange(out_late, in_late, 1, 8)

    for copy in halo2_cols:
        copy.wait_recv()
    wait_rows(*halo2_rows)
    merge(edge2b, from_eb, from_wb)
    unfold(x1, fold1, 1, levels)
    lax.fori_loop(1, levels, lambda k, s: level(x1, k, edge2b, s, store2), carry)
    stores = []
    for f in range(4):
        dst = (tracers_out if f < 2 else velocity_out).at[f % 2]
        stores.append(pltpu.make_async_copy(x2.at[:, f], dst, out_sem.at[f]))
        stores[-1].start()

    early_all.wait_recv()
    tile = (cols // 8, 8, cols)
    sub3 = iota(tile, 1)
    lane3 = iota(tile, 2)
    keep = (sub3 // 2) == (lane3 // ATM_ROWS)
    wanted = (lax.rem(lane3, ATM_ROWS) + 1).astype(f32)
    for j in range(devices * 8 // cols):
        got = in_early[tile[0] * j : tile[0] * (j + 1)]
        ids = jnp.where((sub3 // 2) == 1, got, 0.0)
        ids = (ids + pltpu.roll(ids, 2, 1)) + (pltpu.roll(ids, 4, 1) + pltpu.roll(ids, 6, 1))
        hit = jnp.where(keep & (ids == wanted), 1.0, 0.0)
        row_hot[:, cols * j : cols * (j + 1)] = hit.reshape(cols, cols).T.astype(bf16)
    wets = jnp.where(iota((devices, 8, cols), 1) < 2, in_early[...], 0.0)
    cover = dot(row_hot[0:ATM_ROWS, :], wets.reshape(devices * 8, cols).astype(bf16))
    cover_v[...] = cover
    share = 1.0 / jnp.maximum(cover, 1.0)
    stores.append(pltpu.make_async_copy(cover_v, cover_out, out_sem.at[4]))
    stores[-1].start()

    late_all.wait_recv()
    placed = row_hot[...]
    sums = sum(dot(placed, piece) for piece in split3(in_late[...].reshape(devices * 8, cols)))
    surf_v[...] = sums.reshape(4, ATM_ROWS, cols) * share
    stores.append(pltpu.make_async_copy(surf_v, surface_out, out_sem.at[5]))
    stores[-1].start()

    drain_rows(*halo0_rows)
    drain_rows(*wet_rows)
    drain_rows(*halo1_rows)
    drain_rows(*halo2_rows)
    for copy in halo0_cols + wet_cols + halo1_cols + halo2_cols:
        copy.wait_send()
    early_all.wait_send()
    late_all.wait_send()
    for store in stores:
        store.wait()


def local(tracers, velocity, land_mask, mixing, owners, atm_row):
    n_lon, n_lat = lax.axis_size("lon"), lax.axis_size("lat")
    levels = tracers.shape[1]
    rows, cols = land_mask.shape
    devices = n_lon * n_lat
    blocks = rows * cols // 128
    assert cols == 128 and blocks == rows and ATM_ROWS == 32
    any_spec = pl.BlockSpec(memory_space=pl.ANY)
    vmem = lambda *shape: pltpu.VMEM(shape, f32)
    tile = vmem(rows, cols)
    padded = rows + 16
    scratch = (
        [vmem(levels, 4, padded, cols)] * 2
        + [vmem(levels, 4, rows, cols), vmem(padded, cols)]
        + [pltpu.VMEM((rows, cols), jnp.int32), tile]
        + [pltpu.VMEM((1, blocks), jnp.int32)] * 2
        + [tile] * 14
        + [vmem(levels, 4, cols), vmem(1, cols), vmem(levels, 4, cols)]
        + [vmem(12, rows, cols), pltpu.VMEM((devices * 8, cols), bf16)]
        + [vmem(devices, 8, cols)] * 4
        + [pltpu.VMEM((4 * ATM_ROWS, devices * 8), bf16), tile, vmem(4, ATM_ROWS, cols)]
        + [pltpu.SemaphoreType.DMA((8,)), pltpu.SemaphoreType.DMA((6,))]
        + [pltpu.SemaphoreType.DMA((16,))] * 2
        + [pltpu.SemaphoreType.DMA((2,))] * 2
        + [pltpu.SemaphoreType.REGULAR]
    )
    return pl.pallas_call(
        functools.partial(kernel, n_lon, n_lat, levels, rows, cols),
        out_shape=(
            jax.ShapeDtypeStruct(tracers.shape, f32),
            jax.ShapeDtypeStruct(velocity.shape, f32),
            jax.ShapeDtypeStruct((4, ATM_ROWS, cols), f32),
            jax.ShapeDtypeStruct((ATM_ROWS, cols), f32),
        ),
        in_specs=[any_spec] * 6,
        out_specs=(any_spec,) * 4,
        scratch_shapes=scratch,
        compiler_params=pltpu.CompilerParams(collective_id=0, has_side_effects=True),
        name="ocean",
    )(tracers, velocity, land_mask, mixing, owners.reshape(1, blocks), atm_row.reshape(1, blocks))


def solution(mesh):
    in_specs = (
        P(None, None, "lat", "lon"),
        P(None, None, "lat", "lon"),
        P("lat", "lon"),
        P("lat", "lon"),
        P(("lon", "lat"), None),
        P(("lon", "lat")),
    )
    out_specs = (
        P(None, None, "lat", "lon"),
        P(None, None, "lat", "lon"),
        P(None, ("lon", "lat"), None),
        P(("lon", "lat"), None),
    )
    return jax.shard_map(local, mesh=mesh, in_specs=in_specs, out_specs=out_specs, check_vma=False)
```

time: 219 us -> 36 us (0.16); the launches traced: 216 us -> 35.8 us
  local copies, waits for them, and re-layouts: 84.7 us -> 4.11 us
  starting transfers between devices: 63.3 us -> 0 us
  other arithmetic: 48.9 us -> 0 us
  Pallas kernels: 0 us -> 31 us
  waiting for transfers between devices: 16.9 us -> 0 us
    ppermute x14 -> x0, starting transfers between devices: 38.9 us -> none  [the longest x4 16.8 us: extended(): after = lax.ppermute(leading, axis, down)]
    slice x42 -> x0, local copies, waits for them, and re-layouts: 32.4 us -> none  [the longest x7 8.53 us: neighbour(): rolled = jnp.roll(center, shift, axis=axis)]
    pallas_call x0 -> x1, Pallas kernels: none -> 31 us  [local(): pl.pallas_call(functools.partial(kernel, n_lon, n_lat, levels, rows, cols...]
    all_to_all x2 -> x0, starting transfers between devices: 24.4 us -> none  [exchange_both(): lax.all_to_all(pieces, axis, split_axis=0, concat_axis=0, tiled=True)]
    select_n x18 -> x0, other arithmetic: 16.9 us -> none  [the longest x15 15.1 us: neighbour(): return jnp.where(position, jnp.expand_dims(edge_value, axis), rolled)]
    unnamed x195 -> x10, local copies, waits for them, and re-layouts: 20.3 us -> 4.11 us
    all_to_all x2 -> x0, waiting for transfers between devices: 13.4 us -> none  [exchange_both(): lax.all_to_all(pieces, axis, split_axis=0, concat_axis=0, tiled=True)]
    mul x10 -> x0, other arithmetic: 10.9 us -> none  [the longest x2 5.4 us: local(): 0.5 * (zonal_vel * (fields_east - fields_west) + merid_vel * (fields_nort...]
  transfers between devices with their start and end apart: 16 -> 0, of which waited for: 5 -> 0; matrix products, arithmetic and copies ran while one was open for 50% -> 0% of each run, Pallas kernels for 0% -> 0%
where the time goes in v1:
time: 36 us; the launch traced here: 35.8 us
  Pallas kernels  31 us (86%)
  local copies, waits for them, and re-layouts  4.11 us (11%)
  between operations  0.65 us (2%)
    pallas_call x1, Pallas kernels, local(): pl.pallas_call(functools.partial(kernel, n_lon, n_lat, levels, rows, cols...  31 us
    unnamed x10, local copies, waits for them, and re-layouts  4.11 us

profile of v1, /device:TPU:1, one launch (start us, length us, event | category | flops | bytes accessed | tf_op | source)
XLA Modules:
  0.0 35.8 jit_solution(4356611357194183861)
XLA Ops:
  0.6 31.0 %ocean.1 = (f32[2,16,32,128]{3,2,1,0:T(8,128)}, f32[2,16,32,128]{3,2,1,0:T(8,128)}, f32[4,32,128]{2,1,0:T(8,128)}, f32[32,128]{1,0:T(8,128)}) custom-call(f32[2,16,32,128]{3,2,1,0:T(8,128)} %tracers.1, f32[2,16,32,128]{3,2,1,0:T(8,128)} %velocity.1, s32[32,128]{1,0:T(8,128)} %land_mask.1, f32[32,128]{1,0:T(8,128)} %mixing.1, s32[1,32]{1,0:T(1,128)} %bitcast.2, ...), custom_call_target="tpu_custom_call" | custom-call | tf_op jit(solution)/shard_map/ocean/pallas_call | solution.py:448
  31.6 0.0 copy-start
  31.7 1.9 %copy.14 = f32[2,16,32,128]{3,2,1,0:T(8,128)} copy(f32[2,16,32,128]{3,2,1,0:T(8,128)} %get-tuple-element.8) | data formatting | bytes 1048576
  33.6 0.0 copy-done
  33.6 0.0 copy-start.1
  33.6 0.8 %copy.15 = f32[2,16,32,128]{3,2,1,0:T(8,128)} copy(f32[2,16,32,128]{3,2,1,0:T(8,128)S(1)} %copy-done) | data formatting | bytes 1048576
  34.4 0.1 copy-done.1
  34.4 0.0 copy-start.2
  34.4 0.6 %copy.16 = f32[4,32,128]{2,1,0:T(8,128)} copy(f32[4,32,128]{2,1,0:T(8,128)S(1)} %copy-done.1) | data formatting | bytes 131072
  35.1 0.1 copy-done.2
  35.2 0.6 %copy.17 = f32[32,128]{1,0:T(8,128)} copy(f32[32,128]{1,0:T(8,128)S(1)} %copy-done.2) | data formatting | bytes 32768
Async XLA Ops:
  31.6 1.9 %copy-start = (f32[2,16,32,128]{3,2,1,0:T(8,128)S(1)}, f32[2,16,32,128]{3,2,1,0:T(8,128)}, u32[]{:S(2)}) copy-start(f32[2,16,32,128]{3,2,1,0:T(8,128)} %get-tuple-element.9) | copy-start | bytes 1572868
  33.6 0.9 %copy-start.1 = (f32[4,32,128]{2,1,0:T(8,128)S(1)}, f32[4,32,128]{2,1,0:T(8,128)}, u32[]{:S(2)}) copy-start(f32[4,32,128]{2,1,0:T(8,128)} %get-tuple-element.10) | copy-start | bytes 196612
  34.4 0.7 %copy-start.2 = (f32[32,128]{1,0:T(8,128)S(1)}, f32[32,128]{1,0:T(8,128)}, u32[]{:S(2)}) copy-start(f32[32,128]{1,0:T(8,128)} %get-tuple-element.11) | copy-start | bytes 49156

commit v2 on v1

--- a/solution.py
+++ b/solution.py
@@ -56,12 +56,12 @@
 def kernel(
     n_lon, n_lat, levels, rows, cols,
     tracers, velocity, land_mask, mixing, owners, atm_row,
-    tracers_out, velocity_out, surface_out, cover_out,
-    x0, x1, x2, wet_pad, mask_i, mix_v, own_v, row_v,
+    x2, surf_v, cover_v,
+    x0, x1, wet_pad, mask_i, mix_v, own_v, row_v,
     pack0, pack1a, pack1b, from_e0, from_w0, from_ea, from_wa, from_eb, from_wb, wet_e, wet_w,
     edge0, edge2a, edge2b, fold0, fold_wet, fold1,
-    coef, onehot, out_early, in_early, out_late, in_late, row_hot, cover_v, surf_v,
-    in_sem, out_sem, h_send, h_recv, a_send, a_recv, ready,
+    coef, onehot, out_early, in_early, out_late, in_late, row_hot,
+    in_sem, h_send, h_recv, a_send, a_recv, ready,
 ):
     devices = n_lon * n_lat
     lon = lax.axis_index("lon")
@@ -330,11 +330,8 @@
                 device_id=(peer // n_lat, lax.rem(peer, n_lat)), device_id_type=MESH,
             )
 
-        def go(d, _):
+        for d in range(1, devices):
             copy(d).start()
-            return 0
-
-        lax.fori_loop(1, devices, go, 0)
         return pltpu.make_async_remote_copy(
             src_ref=out.at[0 : devices - 1, 0:height, :], dst_ref=into.at[0 : devices - 1, 0:height, :],
             send_sem=a_send.at[sem], recv_sem=a_recv.at[sem],
@@ -375,12 +372,6 @@
     merge(edge2b, from_eb, from_wb)
     unfold(x1, fold1, 1, levels)
     lax.fori_loop(1, levels, lambda k, s: level(x1, k, edge2b, s, store2), carry)
-    stores = []
-    for f in range(4):
-        dst = (tracers_out if f < 2 else velocity_out).at[f % 2]
-        stores.append(pltpu.make_async_copy(x2.at[:, f], dst, out_sem.at[f]))
-        stores[-1].start()
-
     early_all.wait_recv()
     tile = (cols // 8, 8, cols)
     sub3 = iota(tile, 1)
@@ -397,15 +388,11 @@
     cover = dot(row_hot[0:ATM_ROWS, :], wets.reshape(devices * 8, cols).astype(bf16))
     cover_v[...] = cover
     share = 1.0 / jnp.maximum(cover, 1.0)
-    stores.append(pltpu.make_async_copy(cover_v, cover_out, out_sem.at[4]))
-    stores[-1].start()
 
     late_all.wait_recv()
     placed = row_hot[...]
     sums = sum(dot(placed, piece) for piece in split3(in_late[...].reshape(devices * 8, cols)))
     surf_v[...] = sums.reshape(4, ATM_ROWS, cols) * share
-    stores.append(pltpu.make_async_copy(surf_v, surface_out, out_sem.at[5]))
-    stores[-1].start()
 
     drain_rows(*halo0_rows)
     drain_rows(*wet_rows)
@@ -415,6 +402,17 @@
         copy.wait_send()
     early_all.wait_send()
     late_all.wait_send()
+
+
+def write_out(x2, surf_v, cover_v, tracers_out, velocity_out, surface_out, cover_out, sem):
+    stores = []
+    for f in range(4):
+        dst = (tracers_out if f < 2 else velocity_out).at[f % 2]
+        stores.append(pltpu.make_async_copy(x2.at[:, f], dst, sem.at[f]))
+    stores.append(pltpu.make_async_copy(cover_v, cover_out, sem.at[4]))
+    stores.append(pltpu.make_async_copy(surf_v, surface_out, sem.at[5]))
+    for store in stores:
+        store.start()
     for store in stores:
         store.wait()
 
@@ -432,33 +430,40 @@
     padded = rows + 16
     scratch = (
         [vmem(levels, 4, padded, cols)] * 2
-        + [vmem(levels, 4, rows, cols), vmem(padded, cols)]
+        + [vmem(padded, cols)]
         + [pltpu.VMEM((rows, cols), jnp.int32), tile]
         + [pltpu.VMEM((1, blocks), jnp.int32)] * 2
         + [tile] * 14
         + [vmem(levels, 4, cols), vmem(1, cols), vmem(levels, 4, cols)]
         + [vmem(12, rows, cols), pltpu.VMEM((devices * 8, cols), bf16)]
         + [vmem(devices, 8, cols)] * 4
-        + [pltpu.VMEM((4 * ATM_ROWS, devices * 8), bf16), tile, vmem(4, ATM_ROWS, cols)]
-        + [pltpu.SemaphoreType.DMA((8,)), pltpu.SemaphoreType.DMA((6,))]
+        + [pltpu.VMEM((4 * ATM_ROWS, devices * 8), bf16)]
+        + [pltpu.SemaphoreType.DMA((8,))]
         + [pltpu.SemaphoreType.DMA((16,))] * 2
         + [pltpu.SemaphoreType.DMA((2,))] * 2
         + [pltpu.SemaphoreType.REGULAR]
     )
+    held = pl.pallas_call(
+        functools.partial(kernel, n_lon, n_lat, levels, rows, cols),
+        out_shape=(vmem(levels, 4, rows, cols), vmem(4, ATM_ROWS, cols), vmem(ATM_ROWS, cols)),
+        in_specs=[any_spec] * 6,
+        scratch_shapes=scratch,
+        compiler_params=pltpu.CompilerParams(collective_id=0, has_side_effects=True),
+        name="ocean",
+    )(tracers, velocity, land_mask, mixing, owners.reshape(1, blocks), atm_row.reshape(1, blocks))
     return pl.pallas_call(
-        functools.partial(kernel, n_lon, n_lat, levels, rows, cols),
+        write_out,
         out_shape=(
             jax.ShapeDtypeStruct(tracers.shape, f32),
             jax.ShapeDtypeStruct(velocity.shape, f32),
             jax.ShapeDtypeStruct((4, ATM_ROWS, cols), f32),
             jax.ShapeDtypeStruct((ATM_ROWS, cols), f32),
         ),
-        in_specs=[any_spec] * 6,
+        in_specs=[pl.BlockSpec(memory_space=pltpu.VMEM)] * 3,
         out_specs=(any_spec,) * 4,
-        scratch_shapes=scratch,
-        compiler_params=pltpu.CompilerParams(collective_id=0, has_side_effects=True),
-        name="ocean",
-    )(tracers, velocity, land_mask, mixing, owners.reshape(1, blocks), atm_row.reshape(1, blocks))
+        scratch_shapes=[pltpu.SemaphoreType.DMA((6,))],
+        name="write_out",
+    )(*(pltpu.with_memory_space_constraint(x, pltpu.VMEM) for x in held))
 
 
 def solution(mesh):

time: 36 us -> 30.3 us (0.84)
  local copies, waits for them, and re-layouts: 4.11 us -> 0 us
  Pallas kernels: 31 us -> 29.5 us
    unnamed x10 -> x0, local copies, waits for them, and re-layouts: 4.11 us -> none
    pallas_call x1, Pallas kernels: 31 us -> 28.5 us  [local(): pl.pallas_call(functools.partial(kernel, n_lon, n_lat, levels, rows, cols...]
    pallas_call x0 -> x1, Pallas kernels: none -> 1.04 us  [local(): pl.pallas_call(write_out, out_shape=(jax.ShapeDtypeStruct(tracers.shape,...]
where the time goes in v2:
time: 30.3 us; the launch traced here: 30.1 us
  Pallas kernels  29.5 us (97%)
  between operations  0.64 us (2%)
    pallas_call x1, Pallas kernels, local(): pl.pallas_call(functools.partial(kernel, n_lon, n_lat, levels, rows, cols...  28.5 us
    pallas_call x1, Pallas kernels, local(): pl.pallas_call(write_out, out_shape=(jax.ShapeDtypeStruct(tracers.shape,...  1.04 us

profile of v2, /device:TPU:1, one launch (start us, length us, event | category | flops | bytes accessed | tf_op | source)
XLA Modules:
  0.0 30.1 jit_solution(173256117343600976)
XLA Ops:
  0.6 28.5 %ocean.1 = (f32[16,4,32,128]{3,2,1,0:T(8,128)S(1)}, f32[4,32,128]{2,1,0:T(8,128)S(1)}, f32[32,128]{1,0:T(8,128)S(1)}) custom-call(f32[2,16,32,128]{3,2,1,0:T(8,128)} %tracers.1, f32[2,16,32,128]{3,2,1,0:T(8,128)} %velocity.1, s32[32,128]{1,0:T(8,128)} %land_mask.1, f32[32,128]{1,0:T(8,128)} %mixing.1, s32[1,32]{1,0:T(1,128)} %bitcast.2, s32[1,32]{1,0:T(1,128)} %bitcast.3), custom_call_target="tpu_custom_call" | custom-call | tf_op jit(solution)/shard_map/ocean/pallas_call | solution.py:446
  29.1 1.0 %write_out.1 = (f32[2,16,32,128]{3,2,1,0:T(8,128)}, f32[2,16,32,128]{3,2,1,0:T(8,128)}, f32[4,32,128]{2,1,0:T(8,128)}, f32[32,128]{1,0:T(8,128)}) custom-call(f32[16,4,32,128]{3,2,1,0:T(8,128)S(1)} %get-tuple-element.7.x2, f32[4,32,128]{2,1,0:T(8,128)S(1)} %get-tuple-element.8.surf_v, f32[32,128]{1,0:T(8,128)S(1)} %get-tuple-element.9.cover_v), custom_call_target="tpu_custom_call" | custom-call | tf_op jit(solution)/shard_map/write_out/pallas_call | solution.py:454

commit v3 on v2

--- a/solution.py
+++ b/solution.py
@@ -16,6 +16,8 @@
 VISCOSITY = 0.2
 CORIOLIS_MAX = 0.3
 ATM_ROWS = 32
+UNROLL1, UNROLL2 = 2, 3
+PIECES = 3
 
 MESH = pl.DeviceIdType.MESH
 ROW0 = 8
@@ -27,7 +29,7 @@
     return lax.broadcasted_iota(jnp.int32, shape, dim)
 
 
-def split3(x):
+def split(x):
     hi = x.astype(bf16)
     rest = x - hi.astype(f32)
     mid = rest.astype(bf16)
@@ -54,14 +56,14 @@
 
 
 def kernel(
-    n_lon, n_lat, levels, rows, cols,
+    n_lon, n_lat, levels, rows, cols, offsets,
     tracers, velocity, land_mask, mixing, owners, atm_row,
     x2, surf_v, cover_v,
     x0, x1, wet_pad, mask_i, mix_v, own_v, row_v,
-    pack0, pack1a, pack1b, from_e0, from_w0, from_ea, from_wa, from_eb, from_wb, wet_e, wet_w,
-    edge0, edge2a, edge2b, fold0, fold_wet, fold1,
+    pack0, pack1b, from_e0, from_w0, from_eb, from_wb, edge0, edge2b, rim, rim_e, rim_w, rim_new,
+    rim_pad, fold0, fold1, own_up, up, down, r_s, r_se, r_sw, r_n, r_ne, r_nw,
     coef, onehot, out_early, in_early, out_late, in_late, row_hot,
-    in_sem, h_send, h_recv, a_send, a_recv, ready,
+    in_sem, c_send, c_recv, h_send, h_recv, a_send, a_recv, ready,
 ):
     devices = n_lon * n_lat
     lon = lax.axis_index("lon")
@@ -94,6 +96,11 @@
     for d in range(1, n_lat):
         pl.semaphore_signal(barrier, inc=1, device_id=(lon, lax.rem(lat + d, n_lat)), device_id_type=MESH)
 
+    lat_n, lat_s = lax.rem(lat + 1, n_lat), lax.rem(lat + top, n_lat)
+    for lon_to in (east[0], west[0]):
+        for lat_to in (lat_n, lat_s):
+            pl.semaphore_signal(barrier, inc=1, device_id=(lon_to, lat_to), device_id_type=MESH)
+
     lane8 = iota((8, cols), 1)
     lane = iota((rows, cols), 1)
     first = lane8 == 0
@@ -121,62 +128,124 @@
                 tiles[c] = packed(tiles[c], q, 4 * k + f)
         return tuple(tiles)
 
-    tiles = lax.fori_loop(0, levels, prepare, tuple(jnp.zeros((8, cols), f32) for _ in range(chunks)))
+    empty = tuple(jnp.zeros((8, cols), f32) for _ in range(chunks))
+    tiles = lax.fori_loop(0, levels, prepare, empty, unroll=2)
     for c in range(chunks):
         pack0[8 * c : 8 * c + 8, :] = tiles[c]
+
+    loads[1].wait()
+    rate_t = TIMESTEP * mix_v[...]
+    rate_v = jnp.full((rows, cols), TIMESTEP * VISCOSITY, f32)
+    group = lane // 4
+    packed_rim = jnp.zeros((rows, cols), f32)
+    quantities = [x0[k, f, ROW0:end, :] for k in range(2) for f in range(4)]
+    quantities += [wet] * 4 + [rate_t, rate_t, rate_v, rate_v]
+    for i, value in enumerate(quantities):
+        packed_rim = jnp.where(group == i, pltpu.roll(value, 4 * i + 2, 1), packed_rim)
+    rim[...] = packed_rim
+    for buf, edge, second in ((own_up, end - 1, end - 2), (down, ROW0, ROW0 + 1)):
+        for f in range(4):
+            buf[f : f + 1, :] = x0[0, f, edge : edge + 1, :]
+            buf[4 + f : 5 + f, :] = x0[0, f, second : second + 1, :]
+            buf[8 + f : 9 + f, :] = x0[1, f, edge : edge + 1, :]
+        buf[12:13, :] = wet_pad[edge : edge + 1, :]
+        buf[13:14, :] = wet_pad[second : second + 1, :]
+        buf[14:15, :] = mix_v[edge - ROW0 : edge - ROW0 + 1, :]
+        buf[15:16, :] = rim[edge - ROW0 : edge - ROW0 + 1, :]
+    up[...] = own_up[...]
+
+    @pl.when(lat == top)
+    def _():
+        raw = own_up[...]
+        turned = reverse_lanes(raw)
+        sub16, lane16 = iota((16, cols), 0), iota((16, cols), 1)
+        swapped = jnp.where(lane16 % 4 == 1, pltpu.roll(raw, cols - 1, 1), pltpu.roll(raw, 1, 1))
+        turned = jnp.where(sub16 == 15, swapped, turned)
+        which = jnp.where(sub16 == 15, lane16 // 4, sub16)
+        turned = jnp.where((which < jnp.where(sub16 == 15, 8, 12)) & (which % 4 >= 2), -turned, turned)
+        up[...] = turned
 
     @pl.when(lat == 0)
     def _():
         x0[:, :, ROW0 - 1, :] = jnp.zeros((levels, 4, cols), f32)
         x1[:, :, ROW0 - 1, :] = jnp.zeros((levels, 4, cols), f32)
-        wet_pad[ROW0 - 1 : ROW0, :] = jnp.zeros((1, cols), f32)
-
-    pl.semaphore_wait(barrier, n_lon + n_lat - 2)
-
-    def remote(src, dst, sem, device):
+        for ref in (r_s, r_se, r_sw):
+            ref[...] = jnp.zeros((16, cols), f32)
+
+    pl.semaphore_wait(barrier, n_lon + n_lat + 2)
+
+    def link(src, dst, send_sem, recv_sem, device):
         return pltpu.make_async_remote_copy(
-            src_ref=src, dst_ref=dst, send_sem=h_send.at[sem], recv_sem=h_recv.at[sem],
+            src_ref=src, dst_ref=dst, send_sem=send_sem, recv_sem=recv_sem,
             device_id=device, device_id_type=MESH,
         )
 
+    def remote(src, dst, sem, device):
+        return link(src, dst, h_send.at[sem], h_recv.at[sem], device)
+
+    def first_link(src, dst, send_sem, recv_sem, device):
+        return link(src, dst, c_send.at[send_sem], c_recv.at[recv_sem], device)
+
+    fold_ne = lax.rem(2 * n_lon - 2 - lon, n_lon)
+    fold_nw = lax.rem(n_lon - lon, n_lon)
+    below_top, is_top, above_bottom = lat < top, lat == top, lat > 0
+    ups = [
+        (below_top, first_link(up, r_s, 0, 0, north)),
+        (below_top, first_link(up, r_sw, 1, 2, (east[0], north[1]))),
+        (below_top, first_link(up, r_se, 2, 1, (west[0], north[1]))),
+        (is_top, first_link(up, r_n, 0, 3, mirror)),
+        (is_top & (fold_ne != lon), first_link(up, r_ne, 1, 4, (fold_ne, lat))),
+        (is_top & (fold_nw != lon), first_link(up, r_nw, 2, 5, (fold_nw, lat))),
+    ]
+    downs = [
+        (above_bottom, first_link(down, r_n, 3, 3, south)),
+        (above_bottom, first_link(down, r_nw, 4, 5, (east[0], south[1]))),
+        (above_bottom, first_link(down, r_ne, 5, 4, (west[0], south[1]))),
+    ]
+    sides = [first_link(rim, rim_w, 6, 6, east), first_link(rim, rim_e, 7, 7, west)]
+    for copy in sides:
+        copy.start()
+    for cond, copy in ups + downs:
+        pl.when(cond)(copy.start)
+
+    @pl.when(is_top & (fold_ne == lon))
+    def _():
+        r_ne[...] = up[...]
+
+    @pl.when(is_top & (fold_nw == lon))
+    def _():
+        r_nw[...] = up[...]
+
     def row_copies(x, fold, lo, hi, sem):
         rows_of = lambda ref, r: ref.at[lo:hi, :, r, :]
-        up = remote(rows_of(x, end - 1), rows_of(x, ROW0 - 1), sem, north)
+        ahead = remote(rows_of(x, end - 1), rows_of(x, ROW0 - 1), sem, north)
         over = remote(rows_of(x, end - 1), fold.at[lo:hi], sem + 1, mirror)
-        down = remote(rows_of(x, ROW0), rows_of(x, end), sem + 1, south)
-        return up, over, down
-
-    def start_rows(up, over, down):
-        pl.when(lat < top)(up.start)
+        back = remote(rows_of(x, ROW0), rows_of(x, end), sem + 1, south)
+        return ahead, over, back
+
+    def start_rows(ahead, over, back):
+        pl.when(lat < top)(ahead.start)
         pl.when(lat == top)(over.start)
-        pl.when(lat > 0)(down.start)
-
-    def wait_rows(up, over, down):
-        pl.when(lat > 0)(up.wait_recv)
+        pl.when(lat > 0)(back.start)
+
+    def wait_rows(ahead, over, back):
+        pl.when(lat > 0)(ahead.wait_recv)
         pl.when(lat == top)(over.wait_recv)
-        pl.when(lat < top)(down.wait_recv)
-
-    def drain_rows(up, over, down):
-        pl.when(lat < top)(up.wait_send)
+        pl.when(lat < top)(back.wait_recv)
+
+    def drain_rows(ahead, over, back):
+        pl.when(lat < top)(ahead.wait_send)
         pl.when(lat == top)(over.wait_send)
-        pl.when(lat > 0)(down.wait_send)
+        pl.when(lat > 0)(back.wait_send)
 
     def col_copies(pack, from_w, from_e, sem):
         return remote(pack, from_w, sem, east), remote(pack, from_e, sem + 1, west)
 
-    halo0_rows = row_copies(x0, fold0, 0, levels, 0)
+    halo0_rows = row_copies(x0, fold0, 2, levels, 0)
     halo0_cols = col_copies(pack0, from_w0, from_e0, 2)
-    wet_cols = col_copies(wet_pad.at[ROW0:end, :], wet_w, wet_e, 4)
-    one = lambda ref, r: ref.at[r : r + 1, :]
-    wet_rows = (
-        remote(one(wet_pad, end - 1), one(wet_pad, ROW0 - 1), 6, north),
-        remote(one(wet_pad, end - 1), fold_wet, 7, mirror),
-        remote(one(wet_pad, ROW0), one(wet_pad, end), 7, south),
-    )
     start_rows(*halo0_rows)
-    for copy in halo0_cols + wet_cols:
+    for copy in halo0_cols:
         copy.start()
-    start_rows(*wet_rows)
 
     for d in range(1, n_lat):
         pl.semaphore_signal(ready, inc=1, device_id=(lon, lax.rem(lat + d, n_lat)), device_id_type=MESH)
@@ -194,58 +263,165 @@
     position = jnp.sum(same, axis=0, keepdims=True)
     lane1 = iota((1, cols), 1)
     target = own_lane.astype(jnp.int32) * 8 + (lane1 // blocks) * 2 + position.astype(jnp.int32)
-    onehot[...] = jnp.where(iota((devices * 8, cols), 0) == target, 1.0, 0.0).astype(bf16)
+    hot = jnp.where(iota((devices * 8, cols), 0) == target, 1.0, 0.0).astype(bf16)
+    for j in range(PIECES):
+        onehot[:, cols * j : cols * (j + 1)] = hot
     early = jnp.concatenate(
         [wet, jnp.broadcast_to(row_col, (blocks, cols)), jnp.zeros((2 * blocks, cols), f32)], axis=0
     )
-    out_early[...] = dot(onehot[...], early.astype(bf16)).reshape(devices, 8, cols)
-    in_early[pl.ds(me, 1)] = out_early[pl.ds(me, 1)]
-
-    latitude = (lat * rows + iota((rows, cols), 0)).astype(f32)
-    coriolis = CORIOLIS_MAX * jnp.sin(math.pi * (-0.43 + 0.93 * (latitude + 0.5) / (n_lat * rows)))
-    loads[1].wait()
-
-    for copy in wet_cols:
+    out_early[...] = dot(hot, early.astype(bf16)).reshape(devices, 8, cols)
+    in_early[devices - 1 : devices] = out_early[pl.ds(me, 1)]
+
+    def turning(row):
+        angle = math.pi * (-0.43 + 0.93 * (row.astype(f32) + 0.5) / (n_lat * rows))
+        return CORIOLIS_MAX * jnp.sin(angle)
+
+    coriolis = turning(lat * rows + iota((rows, cols), 0))
+    rim_row = jnp.where(iota((8, cols), 0) < 4, lat * rows - 1, lax.min((lat + 1) * rows, n_lat * rows - 1))
+    coriolis8 = turning(rim_row)
+
+    near = devices // 2
+
+    def exchange(out, into, sem, height):
+        for slot, (a, c) in enumerate(offsets):
+            to_lon, to_lat = lax.rem(lon + a, n_lon), lax.rem(lat + c, n_lat)
+            pltpu.make_async_remote_copy(
+                src_ref=out.at[to_lon * n_lat + to_lat, 0:height, :], dst_ref=into.at[slot, 0:height, :],
+                send_sem=a_send.at[sem], recv_sem=a_recv.at[2 * sem + slot // near],
+                device_id=(to_lon, to_lat), device_id_type=MESH,
+            ).start()
+        parts = []
+        for lo, hi, half in ((0, near, 0), (near, devices - 1, 1)):
+            span = lambda ref: ref.at[lo:hi, 0:height, :]
+            parts.append(pltpu.make_async_remote_copy(
+                src_ref=span(out), dst_ref=span(into),
+                send_sem=a_send.at[sem], recv_sem=a_recv.at[2 * sem + half],
+                device_id=east, device_id_type=MESH,
+            ))
+        return parts
+
+    pl.semaphore_wait(ready, n_lat - 1)
+    early_all = exchange(out_early, in_early, 0, 4)
+
+    for copy in sides:
         copy.wait_recv()
-    wait_rows(*wet_rows)
-
-    @pl.when(lat == top)
-    def _():
-        wet_pad[end : end + 1, :] = reverse_lanes(jnp.broadcast_to(fold_wet[...], (8, cols)))[0:1]
-
-    w_east = pltpu.roll(jnp.where(lane == 0, wet_e[...], wet), cols - 1, 1)
-    w_west = pltpu.roll(jnp.where(lane == cols - 1, wet_w[...], wet), 1, 1)
+    arrivals = [
+        (above_bottom, ups[0]), (above_bottom, ups[1]), (above_bottom, ups[2]),
+        (below_top, downs[0]), (below_top, downs[1]), (below_top, downs[2]), (is_top, ups[3]),
+        (is_top & (fold_ne != lon), ups[4]), (is_top & (fold_nw != lon), ups[5]),
+    ]
+    for cond, (_, copy) in arrivals:
+        pl.when(cond)(copy.wait_recv)
+
+    centre = 1.0 - 2.0 * TIMESTEP * VERTICAL_MIX
+    vertical = TIMESTEP * VERTICAL_MIX
+
+    def surface_step(q, e, w, n, s, below, wets, rate, turn, u, v, field, gx, gy):
+        we, ww, wn, ws, wc = wets
+        dx, dy = e - w, n - s
+        extra = jnp.where(
+            field == 2, TIMESTEP * turn * v - (0.25 * TIMESTEP * GRAVITY) * gx(dx),
+            jnp.where(field == 3, -TIMESTEP * turn * u - (0.25 * TIMESTEP * GRAVITY) * gy(dy), 0.0),
+        )
+        spread = (we * e + ww * w) + (wn * n + ws * s)
+        return wc * (
+            q * (centre - rate * (we + ww + wn + ws)) + vertical * (q + below) + rate * spread
+            - (0.5 * TIMESTEP) * (u * dx + v * dy) + extra
+        )
+
+    two = lambda a, b: jnp.concatenate([a, b], axis=0)
+    four = lambda a, b: two(jnp.broadcast_to(a, (4, cols)), jnp.broadcast_to(b, (4, cols)))
+    from_right = lambda x, corner: pltpu.roll(jnp.where(first, corner, x), cols - 1, 1)
+    from_left = lambda x, corner: pltpu.roll(jnp.where(last, corner, x), 1, 1)
+    both = lambda a, b, lo: two(a[lo : lo + 4, :], b[lo : lo + 4, :])
+    line = lambda a, b, i: four(a[i : i + 1, :], b[i : i + 1, :])
+    q8 = both(r_s, r_n, 0)
+    wet8 = line(r_s, r_n, 12)
+    field8 = iota((8, cols), 0) % 4
+    of = lambda x, i: four(x[i : i + 1], x[4 + i : 5 + i])
+    slope = lambda d: HALINE * of(d, 1) - THERMAL * of(d, 0)
+    rows_new = surface_step(
+        q8, from_right(q8, both(r_se, r_ne, 0)), from_left(q8, both(r_sw, r_nw, 0)),
+        two(down[0:4, :], r_n[4:8, :]), two(r_s[4:8, :], own_up[0:4, :]), both(r_s, r_n, 8),
+        (
+            from_right(wet8, line(r_se, r_ne, 12)), from_left(wet8, line(r_sw, r_nw, 12)),
+            four(down[12:13, :], r_n[13:14, :]), four(r_s[13:14, :], own_up[12:13, :]), wet8,
+        ),
+        jnp.where(field8 < 2, TIMESTEP * line(r_s, r_n, 14), TIMESTEP * VISCOSITY),
+        coriolis8, of(q8, 2), of(q8, 3), field8, slope, slope,
+    )
+    for f in range(4):
+        x1[0, f, ROW0 - 1 : ROW0, :] = rows_new[f : f + 1]
+        x1[0, f, end : end + 1, :] = rows_new[4 + f : 5 + f]
+        for k in range(2):
+            x0[k, f, ROW0 - 1 : ROW0, :] = r_s[8 * k + f : 8 * k + f + 1, :]
+            x0[k, f, end : end + 1, :] = r_n[8 * k + f : 8 * k + f + 1, :]
+    wet_pad[ROW0 - 1 : ROW0, :] = r_s[12:13, :]
+    wet_pad[end : end + 1, :] = r_n[12:13, :]
+
+    low = lane % 4 < 2
+    halves = lambda a, b: jnp.where(iota(a.shape, 1) < cols // 2, a, pltpu.roll(b, cols // 2 - 1, 1))
+    own_rim, east_rim, west_rim = rim[...], rim_e[...], rim_w[...]
+    strip = halves(jnp.where(low, west_rim, own_rim), jnp.where(low, own_rim, east_rim))
+    rim_pad[ROW0:end, :] = strip
+    wide = lambda ref: jnp.broadcast_to(ref[15:16, :], (8, cols))
+    rim_pad[ROW0 - 1 : ROW0, :] = halves(wide(r_sw), wide(r_se))[0:1]
+    rim_pad[end : end + 1, :] = halves(wide(r_nw), wide(r_ne))[0:1]
+    strip_n = rim_pad[ROW0 + 1 : end + 1, :]
+    strip_s = rim_pad[ROW0 - 1 : end - 1, :]
+    right = lambda x, d: pltpu.roll(x, (d + cols) % cols, 1)
+    wets = [right(x, -32) for x in (strip_n, strip_s, strip)]
+    field = group % 16
+
+    def spread_field(i):
+        out = strip
+        for f in range(4):
+            if f != i:
+                out = jnp.where(field == f, right(strip, 4 * (f - i)), out)
+        return out
+
+    rim_new[...] = surface_step(
+        strip, right(strip, -1), right(strip, 1), strip_n, strip_s, right(strip, -16),
+        (right(wets[2], -1), right(wets[2], 1), wets[0], wets[1], wets[2]),
+        right(strip, -48), coriolis, spread_field(2), spread_field(3), field,
+        lambda d: HALINE * right(d, 4) - THERMAL * right(d, 8),
+        lambda d: HALINE * right(d, 8) - THERMAL * right(d, 12),
+    )
+
+    at = lambda x, src, dst: pltpu.roll(x, (dst - src + cols) % cols, 1)
+    w_east = pltpu.roll(jnp.where(lane == 0, at(east_rim, 34, 0), wet), cols - 1, 1)
+    w_west = pltpu.roll(jnp.where(lane == cols - 1, at(west_rim, 33, cols - 1), wet), 1, 1)
     w_north = wet_pad[ROW0 + 1 : end + 1, :]
     w_south = wet_pad[ROW0 - 1 : end - 1, :]
     total = w_east + w_west + w_north + w_south
-    centre = 1.0 - 2.0 * TIMESTEP * VERTICAL_MIX
-    for base, rate in ((0, TIMESTEP * mix_v[...]), (5, TIMESTEP * VISCOSITY)):
+    for base, rate in ((0, rate_t), (5, TIMESTEP * VISCOSITY)):
         coef[base] = wet * (centre - rate * total)
         for j, w in enumerate((w_east, w_west, w_north, w_south)):
             coef[base + 1 + j] = wet * (rate * w)
-    coef[10] = (TIMESTEP * VERTICAL_MIX) * wet
+    coef[10] = vertical * wet
     coef[11] = TIMESTEP * coriolis * wet
 
     pressure_rate = 0.5 * TIMESTEP * GRAVITY
     assert abs(pressure_rate - TIMESTEP * VERTICAL_MIX) < 1e-12
 
-    def level(x, k, edge, carry, store):
+    def level(x, k, side_of, carry, store):
         above = lax.max(k - 1, 0) if not isinstance(k, int) else max(k - 1, 0)
         below = lax.min(k + 1, levels - 1) if not isinstance(k, int) else min(k + 1, levels - 1)
         carry = list(carry)
         for c in range(chunks):
-            mid, up, down = part(c), slice(ROW0 + 8 * c + 1, ROW0 + 8 * c + 9), slice(ROW0 + 8 * c - 1, ROW0 + 8 * c + 7)
+            mid = part(c)
+            ahead = slice(ROW0 + 8 * c + 1, ROW0 + 8 * c + 9)
+            behind = slice(ROW0 + 8 * c - 1, ROW0 + 8 * c + 7)
             own = slice(8 * c, 8 * c + 8)
-            halo = edge[own, :]
             q, e, w, n, s = [], [], [], [], []
             for f in range(4):
                 value = x[k, f, mid, :]
-                side = pltpu.roll(halo, lax.rem(2 * cols - 2 * (4 * k + f), cols), 1)
+                side = side_of(own, k, f)
                 q.append(value)
                 e.append(pltpu.roll(jnp.where(first, side, value), cols - 1, 1))
                 w.append(pltpu.roll(jnp.where(last, side, value), 1, 1))
-                n.append(x[k, f, up, :])
-                s.append(x[k, f, down, :])
+                n.append(x[k, f, ahead, :])
+                s.append(x[k, f, behind, :])
             gx = HALINE * (e[1] - w[1]) - THERMAL * (e[0] - w[0])
             gy = HALINE * (n[1] - s[1]) - THERMAL * (n[0] - s[0])
             sx = carry[2 * c] + gx
@@ -291,88 +467,68 @@
                     for f in range(4):
                         x[k + j, f, end : end + 1, :] = pair[4 * j + f : 4 * j + f + 1]
 
+    def packed_side(edge):
+        return lambda own, k, f: pltpu.roll(edge[own, :], lax.rem(2 * cols - 2 * (4 * k + f), cols), 1)
+
+    def rim_side(from_east, lane_e, from_west, lane_w):
+        def side(own, k, f):
+            i = 4 * (4 * k + f)
+            east_value = at(from_east[own, :], lane_e + i, 0)
+            return jnp.where(first, east_value, at(from_west[own, :], lane_w + i, cols - 1))
+
+        return side
+
+    zeros = tuple(jnp.zeros((8, cols), f32) for _ in range(2 * chunks))
+
+    def step1(k, side_of, carry, tiles):
+        tiles = list(tiles)
+
+        def store(k, f, c, value):
+            x1[k, f, part(c), :] = value
+            if tiles:
+                tiles[c] = packed(tiles[c], value, 4 * k + f)
+
+        carry = level(x0, k, side_of, carry, store)
+        return carry, tuple(tiles)
+
+    near_side = rim_side(rim_e, 2, rim_w, 1)
+    carry1, _ = step1(0, near_side, zeros, ())
+    carry1, tiles = step1(1, near_side, carry1, empty)
+
+    def store2(k, f, c, value):
+        x2[k, f, 8 * c : 8 * c + 8, :] = value
+
+    carry2 = level(x1, 0, rim_side(rim_new, 65, rim_new, 1), zeros, store2)
+    surf = x2[0].reshape(4 * rows, cols)
+    late = dot(onehot[...], jnp.concatenate(split(surf), axis=0))
+    out_late[...] = late.reshape(devices, 8, cols)
+    in_late[devices - 1 : devices] = out_late[pl.ds(me, 1)]
+    late_all = exchange(out_late, in_late, 1, 8)
+
     for copy in halo0_cols:
         copy.wait_recv()
     wait_rows(*halo0_rows)
     merge(edge0, from_e0, from_w0)
-    unfold(x0, fold0, 0, levels)
-
-    zeros = tuple(jnp.zeros((8, cols), f32) for _ in range(2 * chunks))
-    empty = [jnp.zeros((8, cols), f32) for _ in range(chunks)]
-
-    def step1(k, carry, tiles):
-        tiles = list(tiles)
-
-        def store(k, f, c, value):
-            x1[k, f, part(c), :] = value
-            tiles[c] = packed(tiles[c], value, 4 * k + f)
-
-        carry = level(x0, k, edge0, carry, store)
-        return carry, tuple(tiles)
-
-    carry, tiles = step1(0, zeros, empty)
-    for c in range(chunks):
-        pack1a[8 * c : 8 * c + 8, :] = tiles[c]
-    halo1_rows = row_copies(x1, fold1, 0, 1, 8)
-    halo1_cols = col_copies(pack1a, from_wa, from_ea, 10)
-    start_rows(*halo1_rows)
-    for copy in halo1_cols:
-        copy.start()
-
-    pl.semaphore_wait(ready, n_lat - 1)
-
-    def exchange(out, into, sem, height):
-        def copy(d):
-            peer = lax.rem(me + d, devices)
-            return pltpu.make_async_remote_copy(
-                src_ref=out.at[peer, 0:height, :], dst_ref=into.at[me, 0:height, :],
-                send_sem=a_send.at[sem], recv_sem=a_recv.at[sem],
-                device_id=(peer // n_lat, lax.rem(peer, n_lat)), device_id_type=MESH,
-            )
-
-        for d in range(1, devices):
-            copy(d).start()
-        return pltpu.make_async_remote_copy(
-            src_ref=out.at[0 : devices - 1, 0:height, :], dst_ref=into.at[0 : devices - 1, 0:height, :],
-            send_sem=a_send.at[sem], recv_sem=a_recv.at[sem],
-            device_id=east, device_id_type=MESH,
-        )
-
-    early_all = exchange(out_early, in_early, 0, 4)
-
-    carry, tiles = lax.fori_loop(1, levels, lambda k, s: step1(k, *s), (carry, tiles))
+    unfold(x0, fold0, 2, levels)
+    _, tiles = lax.fori_loop(
+        2, levels, lambda k, s: step1(k, packed_side(edge0), *s), (carry1, tiles), unroll=UNROLL1
+    )
     for c in range(chunks):
         pack1b[8 * c : 8 * c + 8, :] = tiles[c]
-    halo2_rows = row_copies(x1, fold1, 1, levels, 12)
-    halo2_cols = col_copies(pack1b, from_wb, from_eb, 14)
+    halo2_rows = row_copies(x1, fold1, 1, levels, 4)
+    halo2_cols = col_copies(pack1b, from_wb, from_eb, 6)
     start_rows(*halo2_rows)
     for copy in halo2_cols:
         copy.start()
-
-    for copy in halo1_cols:
-        copy.wait_recv()
-    wait_rows(*halo1_rows)
-    merge(edge2a, from_ea, from_wa)
-    unfold(x1, fold1, 0, 1)
-
-    def store2(k, f, c, value):
-        x2[k, f, 8 * c : 8 * c + 8, :] = value
-
-    carry = level(x1, 0, edge2a, zeros, store2)
-    surf = x2[0].reshape(4 * rows, cols)
-    hot = onehot[...]
-    late = sum(dot(hot, piece) for piece in split3(surf))
-    out_late[...] = late.reshape(devices, 8, cols)
-    in_late[pl.ds(me, 1)] = out_late[pl.ds(me, 1)]
-    late_all = exchange(out_late, in_late, 1, 8)
 
     for copy in halo2_cols:
         copy.wait_recv()
     wait_rows(*halo2_rows)
     merge(edge2b, from_eb, from_wb)
     unfold(x1, fold1, 1, levels)
-    lax.fori_loop(1, levels, lambda k, s: level(x1, k, edge2b, s, store2), carry)
-    early_all.wait_recv()
+    lax.fori_loop(1, levels, lambda k, s: level(x1, k, packed_side(edge2b), s, store2), carry2, unroll=UNROLL2)
+    for copy in early_all:
+        copy.wait_recv()
     tile = (cols // 8, 8, cols)
     sub3 = iota(tile, 1)
     lane3 = iota(tile, 2)
@@ -389,19 +545,27 @@
     cover_v[...] = cover
     share = 1.0 / jnp.maximum(cover, 1.0)
 
-    late_all.wait_recv()
-    placed = row_hot[...]
-    sums = sum(dot(placed, piece) for piece in split3(in_late[...].reshape(devices * 8, cols)))
+    sums = jnp.zeros((4 * ATM_ROWS, cols), f32)
+    for half, copy in enumerate(late_all):
+        copy.wait_recv()
+        got = in_late[near * half : near * (half + 1)].reshape(near * 8, cols)
+        placed = row_hot[:, near * 8 * half : near * 8 * (half + 1)]
+        for piece in split(got):
+            sums = sums + dot(placed, piece)
     surf_v[...] = sums.reshape(4, ATM_ROWS, cols) * share
 
+    for cond, copy in ups + downs:
+        pl.when(cond)(copy.wait_send)
     drain_rows(*halo0_rows)
-    drain_rows(*wet_rows)
-    drain_rows(*halo1_rows)
     drain_rows(*halo2_rows)
-    for copy in halo0_cols + wet_cols + halo1_cols + halo2_cols:
+    for copy in [*sides, *halo0_cols, *halo2_cols]:
         copy.wait_send()
-    early_all.wait_send()
-    late_all.wait_send()
+    whole = lambda ref, height: ref.at[0 : devices - 1, 0:height, :]
+    for sem, (out, into, height) in enumerate(((out_early, in_early, 4), (out_late, in_late, 8))):
+        pltpu.make_async_remote_copy(
+            src_ref=whole(out, height), dst_ref=whole(into, height),
+            send_sem=a_send.at[sem], recv_sem=a_recv.at[2 * sem], device_id=east, device_id_type=MESH,
+        ).wait_send()
 
 
 def write_out(x2, surf_v, cover_v, tracers_out, velocity_out, surface_out, cover_out, sem):
@@ -433,18 +597,25 @@
         + [vmem(padded, cols)]
         + [pltpu.VMEM((rows, cols), jnp.int32), tile]
         + [pltpu.VMEM((1, blocks), jnp.int32)] * 2
-        + [tile] * 14
-        + [vmem(levels, 4, cols), vmem(1, cols), vmem(levels, 4, cols)]
-        + [vmem(12, rows, cols), pltpu.VMEM((devices * 8, cols), bf16)]
+        + [tile] * 12
+        + [vmem(padded, cols)]
+        + [vmem(levels, 4, cols)] * 2
+        + [vmem(16, cols)] * 9
+        + [vmem(12, rows, cols), pltpu.VMEM((devices * 8, PIECES * cols), bf16)]
         + [vmem(devices, 8, cols)] * 4
         + [pltpu.VMEM((4 * ATM_ROWS, devices * 8), bf16)]
         + [pltpu.SemaphoreType.DMA((8,))]
-        + [pltpu.SemaphoreType.DMA((16,))] * 2
-        + [pltpu.SemaphoreType.DMA((2,))] * 2
+        + [pltpu.SemaphoreType.DMA((8,))] * 4
+        + [pltpu.SemaphoreType.DMA((2,)), pltpu.SemaphoreType.DMA((4,))]
         + [pltpu.SemaphoreType.REGULAR]
     )
+    ring = lambda d, size: min(d % size, size - d % size)
+    half_lat = n_lat // 2
+    hops = lambda a, c: ring(a, n_lon // 2) + ring(c // 2, half_lat // 2) + 2 * (a // (n_lon // 2)) + c // half_lat
+    offsets = [(a, c) for a in range(n_lon) for c in range(n_lat) if a or c]
+    offsets.sort(key=lambda o: hops(*o))
     held = pl.pallas_call(
-        functools.partial(kernel, n_lon, n_lat, levels, rows, cols),
+        functools.partial(kernel, n_lon, n_lat, levels, rows, cols, offsets),
         out_shape=(vmem(levels, 4, rows, cols), vmem(4, ATM_ROWS, cols), vmem(ATM_ROWS, cols)),
         in_specs=[any_spec] * 6,
         scratch_shapes=scratch,

time: 30.3 us -> 29 us (0.957)
  Pallas kernels: 29.5 us -> 28.2 us
    pallas_call x1, Pallas kernels: 28.5 us -> 27.1 us  [local(): pl.pallas_call(functools.partial(kernel, n_lon, n_lat, levels, rows, cols...]
where the time goes in v3:
time: 29 us; the launch traced here: 28.8 us
  Pallas kernels  28.2 us (97%)
  between operations  0.64 us (2%)
    pallas_call x1, Pallas kernels, local(): pl.pallas_call(functools.partial(kernel, n_lon, n_lat, levels, rows, cols...  27.1 us
    pallas_call x1, Pallas kernels, local(): pl.pallas_call(write_out, out_shape=(jax.ShapeDtypeStruct(tracers.shape,...  1.04 us

profile of v3, /device:TPU:1, one launch (start us, length us, event | category | flops | bytes accessed | tf_op | source)
XLA Modules:
  0.0 28.8 jit_solution(11622194816459800060)
XLA Ops:
  0.6 27.1 %ocean.1 = (f32[16,4,32,128]{3,2,1,0:T(8,128)S(1)}, f32[4,32,128]{2,1,0:T(8,128)S(1)}, f32[32,128]{1,0:T(8,128)S(1)}) custom-call(f32[2,16,32,128]{3,2,1,0:T(8,128)} %tracers.1, f32[2,16,32,128]{3,2,1,0:T(8,128)} %velocity.1, s32[32,128]{1,0:T(8,128)} %land_mask.1, f32[32,128]{1,0:T(8,128)} %mixing.1, s32[1,32]{1,0:T(1,128)} %bitcast.2, s32[1,32]{1,0:T(1,128)} %bitcast.3), custom_call_target="tpu_custom_call" | custom-call | tf_op jit(solution)/shard_map/ocean/pallas_call | solution.py:617
  27.8 1.0 %write_out.1 = (f32[2,16,32,128]{3,2,1,0:T(8,128)}, f32[2,16,32,128]{3,2,1,0:T(8,128)}, f32[4,32,128]{2,1,0:T(8,128)}, f32[32,128]{1,0:T(8,128)}) custom-call(f32[16,4,32,128]{3,2,1,0:T(8,128)S(1)} %get-tuple-element.7.x2, f32[4,32,128]{2,1,0:T(8,128)S(1)} %get-tuple-element.8.surf_v, f32[32,128]{1,0:T(8,128)S(1)} %get-tuple-element.9.cover_v), custom_call_target="tpu_custom_call" | custom-call | tf_op jit(solution)/shard_map/write_out/pallas_call | solution.py:625

commit v4 on v3

--- a/solution.py
+++ b/solution.py
@@ -61,7 +61,7 @@
     x2, surf_v, cover_v,
     x0, x1, wet_pad, mask_i, mix_v, own_v, row_v,
     pack0, pack1b, from_e0, from_w0, from_eb, from_wb, edge0, edge2b, rim, rim_e, rim_w, rim_new,
-    rim_pad, fold0, fold1, own_up, up, down, r_s, r_se, r_sw, r_n, r_ne, r_nw,
+    rim_pad, fold0, rows_s, rows_n, own_up, up, down, r_s, r_se, r_sw, r_n, r_ne, r_nw,
     coef, onehot, out_early, in_early, out_late, in_late, row_hot,
     in_sem, c_send, c_recv, h_send, h_recv, a_send, a_recv, ready,
 ):
@@ -112,6 +112,9 @@
     def packed(tile, value, i):
         where = (lane8 == 2 * i) | (lane8 == lax.rem(2 * i + cols - 1, cols))
         return jnp.where(where, pltpu.roll(value, 2 * i, 1), tile)
+
+    for row in (ROW0 - 1, end):
+        x1[:, :, row, :] = jnp.zeros((levels, 4, cols), f32)
 
     loads[0].wait()
     wet = mask_i[...].astype(f32)
@@ -168,7 +171,7 @@
     @pl.when(lat == 0)
     def _():
         x0[:, :, ROW0 - 1, :] = jnp.zeros((levels, 4, cols), f32)
-        x1[:, :, ROW0 - 1, :] = jnp.zeros((levels, 4, cols), f32)
+        rows_s[...] = jnp.zeros((levels, 4, cols), f32)
         for ref in (r_s, r_se, r_sw):
             ref[...] = jnp.zeros((16, cols), f32)
 
@@ -216,11 +219,11 @@
     def _():
         r_nw[...] = up[...]
 
-    def row_copies(x, fold, lo, hi, sem):
-        rows_of = lambda ref, r: ref.at[lo:hi, :, r, :]
-        ahead = remote(rows_of(x, end - 1), rows_of(x, ROW0 - 1), sem, north)
-        over = remote(rows_of(x, end - 1), fold.at[lo:hi], sem + 1, mirror)
-        back = remote(rows_of(x, ROW0), rows_of(x, end), sem + 1, south)
+    def row_copies(x, lo, sem, into_s, into_n, into_fold):
+        last_row, first_row = x.at[lo:levels, :, end - 1, :], x.at[lo:levels, :, ROW0, :]
+        ahead = remote(last_row, into_s, sem, north)
+        over = remote(last_row, into_fold, sem + 1, mirror)
+        back = remote(first_row, into_n, sem + 1, south)
         return ahead, over, back
 
     def start_rows(ahead, over, back):
@@ -241,7 +244,9 @@
     def col_copies(pack, from_w, from_e, sem):
         return remote(pack, from_w, sem, east), remote(pack, from_e, sem + 1, west)
 
-    halo0_rows = row_copies(x0, fold0, 2, levels, 0)
+    halo0_rows = row_copies(
+        x0, 2, 0, x0.at[2:levels, :, ROW0 - 1, :], x0.at[2:levels, :, end, :], fold0.at[2:levels]
+    )
     halo0_cols = col_copies(pack0, from_w0, from_e0, 2)
     start_rows(*halo0_rows)
     for copy in halo0_cols:
@@ -454,7 +459,7 @@
     def merge(edge, from_e, from_w):
         edge[...] = jnp.where(lax.rem(lane, 2) == 0, from_e[...], from_w[...])
 
-    def unfold(x, fold, lo, hi):
+    def unfold(fold, lo, hi, put):
         @pl.when(lat == top)
         def _():
             for k in range(lo, hi, 2):
@@ -463,9 +468,7 @@
                 pair = reverse_lanes(pair)
                 field = lax.rem(iota(pair.shape, 0), 4)
                 pair = jnp.where(field < 2, pair, -pair)
-                for j in range(width):
-                    for f in range(4):
-                        x[k + j, f, end : end + 1, :] = pair[4 * j + f : 4 * j + f + 1]
+                put(k, width, pair)
 
     def packed_side(edge):
         return lambda own, k, f: pltpu.roll(edge[own, :], lax.rem(2 * cols - 2 * (4 * k + f), cols), 1)
@@ -509,24 +512,84 @@
         copy.wait_recv()
     wait_rows(*halo0_rows)
     merge(edge0, from_e0, from_w0)
-    unfold(x0, fold0, 2, levels)
+
+    def put_rows(k, width, pair):
+        for j in range(width):
+            for f in range(4):
+                x0[k + j, f, end : end + 1, :] = pair[4 * j + f : 4 * j + f + 1]
+
+    unfold(fold0, 2, levels, put_rows)
     _, tiles = lax.fori_loop(
         2, levels, lambda k, s: step1(k, packed_side(edge0), *s), (carry1, tiles), unroll=UNROLL1
     )
     for c in range(chunks):
         pack1b[8 * c : 8 * c + 8, :] = tiles[c]
-    halo2_rows = row_copies(x1, fold1, 1, levels, 4)
+    halo2_rows = row_copies(
+        x1, 1, 4, rows_s.at[1:levels], rows_n.at[1:levels], rows_n.at[1:levels]
+    )
     halo2_cols = col_copies(pack1b, from_wb, from_eb, 6)
     start_rows(*halo2_rows)
     for copy in halo2_cols:
         copy.start()
 
+    nothing = jnp.zeros((8, cols), f32)
+    lax.fori_loop(
+        1, levels, lambda k, s: level(x1, k, lambda own, k, f: nothing, s, store2), carry2, unroll=UNROLL2
+    )
+
     for copy in halo2_cols:
         copy.wait_recv()
     wait_rows(*halo2_rows)
-    merge(edge2b, from_eb, from_wb)
-    unfold(x1, fold1, 1, levels)
-    lax.fori_loop(1, levels, lambda k, s: level(x1, k, packed_side(edge2b), s, store2), carry2, unroll=UNROLL2)
+    edge2b[...] = jnp.where(
+        lax.rem(lane, 2) == 0, pltpu.roll(from_wb[...], 1, 1), pltpu.roll(from_eb[...], cols - 1, 1)
+    )
+
+    def put_back(k, width, pair):
+        rows_n[k : k + width] = pair.reshape(width, 4, cols)
+
+    unfold(rows_n, 1, levels, put_back)
+
+    def share(k, carry):
+        carry = list(carry)
+        for c in range(chunks):
+            own, mid = slice(8 * c, 8 * c + 8), part(c)
+            u = (0.5 * TIMESTEP) * x1[k, 2, mid, :]
+            v = (0.5 * TIMESTEP) * x1[k, 3, mid, :]
+            vert = coef[10, own, :]
+            side = edge2b[own, :]
+            halo = [pltpu.roll(side, lax.rem(2 * cols - 2 * (4 * k + f), cols), 1) for f in range(4)]
+            gx = HALINE * halo[1] - THERMAL * halo[0]
+            gx = jnp.where(last, gx, jnp.where(first, -gx, 0.0))
+            carry[c] = carry[c] + gx
+            add = []
+            for f in range(4):
+                base = 0 if f < 2 else 5
+                rate = jnp.where(
+                    last, coef[base + 1, own, :] - u, jnp.where(first, coef[base + 2, own, :] + u, 0.0)
+                )
+                add.append(rate * halo[f])
+            add[2] = add[2] - vert * (carry[c] - 0.5 * gx)
+            for outside, rows_of, edge, index, sign in (
+                (c == 0, rows_s, 0, 4, 1.0), (c == chunks - 1, rows_n, 7, 3, -1.0)
+            ):
+                if outside:
+                    here = iota((8, cols), 0) == edge
+                    line_of = [
+                        jnp.where(here, jnp.broadcast_to(rows_of[k, f : f + 1, :], (8, cols)), 0.0)
+                        for f in range(4)
+                    ]
+                    gy = -sign * (HALINE * line_of[1] - THERMAL * line_of[0])
+                    slot = chunks + (0 if c == 0 else 1)
+                    carry[slot] = carry[slot] + gy
+                    for f in range(4):
+                        base = 0 if f < 2 else 5
+                        add[f] = add[f] + (coef[base + index, own, :] + sign * v) * line_of[f]
+                    add[3] = add[3] - vert * (carry[slot] - 0.5 * gy)
+            for f in range(4):
+                x2[k, f, own, :] = x2[k, f, own, :] + add[f]
+        return tuple(carry)
+
+    lax.fori_loop(1, levels, share, (nothing,) * (chunks + 2), unroll=UNROLL2)
     for copy in early_all:
         copy.wait_recv()
     tile = (cols // 8, 8, cols)
@@ -599,7 +662,7 @@
         + [pltpu.VMEM((1, blocks), jnp.int32)] * 2
         + [tile] * 12
         + [vmem(padded, cols)]
-        + [vmem(levels, 4, cols)] * 2
+        + [vmem(levels, 4, cols)] * 3
         + [vmem(16, cols)] * 9
         + [vmem(12, rows, cols), pltpu.VMEM((devices * 8, PIECES * cols), bf16)]
         + [vmem(devices, 8, cols)] * 4

time: 29 us -> 28 us (0.966)
  Pallas kernels: 28.2 us -> 27.2 us
    pallas_call x1, Pallas kernels: 27.1 us -> 26.2 us  [local(): pl.pallas_call(functools.partial(kernel, n_lon, n_lat, levels, rows, cols...]
where the time goes in v4:
time: 28 us; the launch traced here: 27.9 us
  Pallas kernels  27.2 us (97%)
  between operations  0.64 us (2%)
    pallas_call x1, Pallas kernels, local(): pl.pallas_call(functools.partial(kernel, n_lon, n_lat, levels, rows, cols...  26.2 us
    pallas_call x1, Pallas kernels, local(): pl.pallas_call(write_out, out_shape=(jax.ShapeDtypeStruct(tracers.shape,...  1.04 us

profile of v4, /device:TPU:1, one launch (start us, length us, event | category | flops | bytes accessed | tf_op | source)
XLA Modules:
  0.0 27.9 jit_solution(17796861202329925472)
XLA Ops:
  0.6 26.2 %ocean.1 = (f32[16,4,32,128]{3,2,1,0:T(8,128)S(1)}, f32[4,32,128]{2,1,0:T(8,128)S(1)}, f32[32,128]{1,0:T(8,128)S(1)}) custom-call(f32[2,16,32,128]{3,2,1,0:T(8,128)} %tracers.1, f32[2,16,32,128]{3,2,1,0:T(8,128)} %velocity.1, s32[32,128]{1,0:T(8,128)} %land_mask.1, f32[32,128]{1,0:T(8,128)} %mixing.1, s32[1,32]{1,0:T(1,128)} %bitcast.2, s32[1,32]{1,0:T(1,128)} %bitcast.3), custom_call_target="tpu_custom_call" | custom-call | tf_op jit(solution)/shard_map/ocean/pallas_call | solution.py:680
  26.8 1.0 %write_out.1 = (f32[2,16,32,128]{3,2,1,0:T(8,128)}, f32[2,16,32,128]{3,2,1,0:T(8,128)}, f32[4,32,128]{2,1,0:T(8,128)}, f32[32,128]{1,0:T(8,128)}) custom-call(f32[16,4,32,128]{3,2,1,0:T(8,128)S(1)} %get-tuple-element.7.x2, f32[4,32,128]{2,1,0:T(8,128)S(1)} %get-tuple-element.8.surf_v, f32[32,128]{1,0:T(8,128)S(1)} %get-tuple-element.9.cover_v), custom_call_target="tpu_custom_call" | custom-call | tf_op jit(solution)/shard_map/write_out/pallas_call | solution.py:688

commit v5 on v4

--- a/solution.py
+++ b/solution.py
@@ -84,9 +84,10 @@
         pltpu.make_async_copy(owners, own_v, in_sem.at[2]),
         pltpu.make_async_copy(atm_row, row_v, in_sem.at[3]),
     ]
-    for f in range(4):
-        src = (tracers if f < 2 else velocity).at[f % 2]
-        loads.append(pltpu.make_async_copy(src, x0.at[:, f, ROW0:end, :], in_sem.at[4 + f]))
+    for lo, hi, sem in ((0, 2, 4), (2, levels, 8)):
+        for f in range(4):
+            src = (tracers if f < 2 else velocity).at[f % 2, lo:hi]
+            loads.append(pltpu.make_async_copy(src, x0.at[lo:hi, f, ROW0:end, :], in_sem.at[sem + f]))
     for load in loads:
         load.start()
 
@@ -119,7 +120,7 @@
     loads[0].wait()
     wet = mask_i[...].astype(f32)
     wet_pad[ROW0:end, :] = wet
-    for load in loads[4:]:
+    for load in loads[4:8]:
         load.wait()
 
     def prepare(k, tiles):
@@ -132,9 +133,7 @@
         return tuple(tiles)
 
     empty = tuple(jnp.zeros((8, cols), f32) for _ in range(chunks))
-    tiles = lax.fori_loop(0, levels, prepare, empty, unroll=2)
-    for c in range(chunks):
-        pack0[8 * c : 8 * c + 8, :] = tiles[c]
+    packs = prepare(1, prepare(0, empty))
 
     loads[1].wait()
     rate_t = TIMESTEP * mix_v[...]
@@ -244,6 +243,14 @@
     def col_copies(pack, from_w, from_e, sem):
         return remote(pack, from_w, sem, east), remote(pack, from_e, sem + 1, west)
 
+    for d in range(1, n_lat):
+        pl.semaphore_signal(ready, inc=1, device_id=(lon, lax.rem(lat + d, n_lat)), device_id_type=MESH)
+
+    for load in loads[8:]:
+        load.wait()
+    tiles = lax.fori_loop(2, levels, prepare, packs, unroll=2)
+    for c in range(chunks):
+        pack0[8 * c : 8 * c + 8, :] = tiles[c]
     halo0_rows = row_copies(
         x0, 2, 0, x0.at[2:levels, :, ROW0 - 1, :], x0.at[2:levels, :, end, :], fold0.at[2:levels]
     )
@@ -251,9 +258,6 @@
     start_rows(*halo0_rows)
     for copy in halo0_cols:
         copy.start()
-
-    for d in range(1, n_lat):
-        pl.semaphore_signal(ready, inc=1, device_id=(lon, lax.rem(lat + d, n_lat)), device_id_type=MESH)
 
     loads[2].wait()
     loads[3].wait()
@@ -537,6 +541,24 @@
         1, levels, lambda k, s: level(x1, k, lambda own, k, f: nothing, s, store2), carry2, unroll=UNROLL2
     )
 
+    for copy in early_all:
+        copy.wait_recv()
+    tile = (cols // 8, 8, cols)
+    sub3 = iota(tile, 1)
+    lane3 = iota(tile, 2)
+    keep = (sub3 // 2) == (lane3 // ATM_ROWS)
+    wanted = (lax.rem(lane3, ATM_ROWS) + 1).astype(f32)
+    for j in range(devices * 8 // cols):
+        got = in_early[tile[0] * j : tile[0] * (j + 1)]
+        ids = jnp.where((sub3 // 2) == 1, got, 0.0)
+        ids = (ids + pltpu.roll(ids, 2, 1)) + (pltpu.roll(ids, 4, 1) + pltpu.roll(ids, 6, 1))
+        hit = jnp.where(keep & (ids == wanted), 1.0, 0.0)
+        row_hot[:, cols * j : cols * (j + 1)] = hit.reshape(cols, cols).T.astype(bf16)
+    wets = jnp.where(iota((devices, 8, cols), 1) < 2, in_early[...], 0.0)
+    cover = dot(row_hot[0:ATM_ROWS, :], wets.reshape(devices * 8, cols).astype(bf16))
+    cover_v[...] = cover
+    share = 1.0 / jnp.maximum(cover, 1.0)
+
     for copy in halo2_cols:
         copy.wait_recv()
     wait_rows(*halo2_rows)
@@ -549,7 +571,7 @@
 
     unfold(rows_n, 1, levels, put_back)
 
-    def share(k, carry):
+    def halo_share(k, carry):
         carry = list(carry)
         for c in range(chunks):
             own, mid = slice(8 * c, 8 * c + 8), part(c)
@@ -589,25 +611,7 @@
                 x2[k, f, own, :] = x2[k, f, own, :] + add[f]
         return tuple(carry)
 
-    lax.fori_loop(1, levels, share, (nothing,) * (chunks + 2), unroll=UNROLL2)
-    for copy in early_all:
-        copy.wait_recv()
-    tile = (cols // 8, 8, cols)
-    sub3 = iota(tile, 1)
-    lane3 = iota(tile, 2)
-    keep = (sub3 // 2) == (lane3 // ATM_ROWS)
-    wanted = (lax.rem(lane3, ATM_ROWS) + 1).astype(f32)
-    for j in range(devices * 8 // cols):
-        got = in_early[tile[0] * j : tile[0] * (j + 1)]
-        ids = jnp.where((sub3 // 2) == 1, got, 0.0)
-        ids = (ids + pltpu.roll(ids, 2, 1)) + (pltpu.roll(ids, 4, 1) + pltpu.roll(ids, 6, 1))
-        hit = jnp.where(keep & (ids == wanted), 1.0, 0.0)
-        row_hot[:, cols * j : cols * (j + 1)] = hit.reshape(cols, cols).T.astype(bf16)
-    wets = jnp.where(iota((devices, 8, cols), 1) < 2, in_early[...], 0.0)
-    cover = dot(row_hot[0:ATM_ROWS, :], wets.reshape(devices * 8, cols).astype(bf16))
-    cover_v[...] = cover
-    share = 1.0 / jnp.maximum(cover, 1.0)
-
+    lax.fori_loop(1, levels, halo_share, (nothing,) * (chunks + 2), unroll=UNROLL2)
     sums = jnp.zeros((4 * ATM_ROWS, cols), f32)
     for half, copy in enumerate(late_all):
         copy.wait_recv()
@@ -667,7 +671,7 @@
         + [vmem(12, rows, cols), pltpu.VMEM((devices * 8, PIECES * cols), bf16)]
         + [vmem(devices, 8, cols)] * 4
         + [pltpu.VMEM((4 * ATM_ROWS, devices * 8), bf16)]
-        + [pltpu.SemaphoreType.DMA((8,))]
+        + [pltpu.SemaphoreType.DMA((12,))]
         + [pltpu.SemaphoreType.DMA((8,))] * 4
         + [pltpu.SemaphoreType.DMA((2,)), pltpu.SemaphoreType.DMA((4,))]
         + [pltpu.SemaphoreType.REGULAR]

time: 28 us -> 27.6 us (0.986)
  Pallas kernels: 27.2 us -> 26.8 us
    pallas_call x1, Pallas kernels: 26.2 us -> 25.7 us  [local(): pl.pallas_call(functools.partial(kernel, n_lon, n_lat, levels, rows, cols...]
where the time goes in v5:
time: 27.6 us; the launch traced here: 27.4 us
  Pallas kernels  26.8 us (97%)
  between operations  0.64 us (2%)
    pallas_call x1, Pallas kernels, local(): pl.pallas_call(functools.partial(kernel, n_lon, n_lat, levels, rows, cols...  25.7 us
    pallas_call x1, Pallas kernels, local(): pl.pallas_call(write_out, out_shape=(jax.ShapeDtypeStruct(tracers.shape,...  1.04 us

profile of v5, /device:TPU:1, one launch (start us, length us, event | category | flops | bytes accessed | tf_op | source)
XLA Modules:
  0.0 27.4 jit_solution(2851025872552611796)
XLA Ops:
  0.6 25.7 %ocean.1 = (f32[16,4,32,128]{3,2,1,0:T(8,128)S(1)}, f32[4,32,128]{2,1,0:T(8,128)S(1)}, f32[32,128]{1,0:T(8,128)S(1)}) custom-call(f32[2,16,32,128]{3,2,1,0:T(8,128)} %tracers.1, f32[2,16,32,128]{3,2,1,0:T(8,128)} %velocity.1, s32[32,128]{1,0:T(8,128)} %land_mask.1, f32[32,128]{1,0:T(8,128)} %mixing.1, s32[1,32]{1,0:T(1,128)} %bitcast.2, s32[1,32]{1,0:T(1,128)} %bitcast.3), custom_call_target="tpu_custom_call" | custom-call | tf_op jit(solution)/shard_map/ocean/pallas_call | solution.py:684
  26.4 1.0 %write_out.1 = (f32[2,16,32,128]{3,2,1,0:T(8,128)}, f32[2,16,32,128]{3,2,1,0:T(8,128)}, f32[4,32,128]{2,1,0:T(8,128)}, f32[32,128]{1,0:T(8,128)}) custom-call(f32[16,4,32,128]{3,2,1,0:T(8,128)S(1)} %get-tuple-element.7.x2, f32[4,32,128]{2,1,0:T(8,128)S(1)} %get-tuple-element.8.surf_v, f32[32,128]{1,0:T(8,128)S(1)} %get-tuple-element.9.cover_v), custom_call_target="tpu_custom_call" | custom-call | tf_op jit(solution)/shard_map/write_out/pallas_call | solution.py:692

commit v6 on v5

--- a/solution.py
+++ b/solution.py
@@ -99,8 +99,11 @@
 
     lat_n, lat_s = lax.rem(lat + 1, n_lat), lax.rem(lat + top, n_lat)
     for lon_to in (east[0], west[0]):
-        for lat_to in (lat_n, lat_s):
-            pl.semaphore_signal(barrier, inc=1, device_id=(lon_to, lat_to), device_id_type=MESH)
+        for has, lat_to in ((lat < top, lat_n), (lat > 0, lat_s)):
+
+            @pl.when(has)
+            def _():
+                pl.semaphore_signal(barrier, inc=1, device_id=(lon_to, lat_to), device_id_type=MESH)
 
     lane8 = iota((8, cols), 1)
     lane = iota((rows, cols), 1)
@@ -174,7 +177,7 @@
         for ref in (r_s, r_se, r_sw):
             ref[...] = jnp.zeros((16, cols), f32)
 
-    pl.semaphore_wait(barrier, n_lon + n_lat + 2)
+    pl.semaphore_wait(barrier, n_lon + n_lat + 2 - 2 * jnp.where((lat == 0) | (lat == top), 1, 0))
 
     def link(src, dst, send_sem, recv_sem, device):
         return pltpu.make_async_remote_copy(
@@ -289,7 +292,7 @@
     rim_row = jnp.where(iota((8, cols), 0) < 4, lat * rows - 1, lax.min((lat + 1) * rows, n_lat * rows - 1))
     coriolis8 = turning(rim_row)
 
-    near = devices // 2
+    near = devices // 8 * 7
 
     def exchange(out, into, sem, height):
         for slot, (a, c) in enumerate(offsets):
@@ -615,8 +618,9 @@
     sums = jnp.zeros((4 * ATM_ROWS, cols), f32)
     for half, copy in enumerate(late_all):
         copy.wait_recv()
-        got = in_late[near * half : near * (half + 1)].reshape(near * 8, cols)
-        placed = row_hot[:, near * 8 * half : near * 8 * (half + 1)]
+        lo, hi = ((0, near), (near, devices))[half]
+        got = in_late[lo:hi].reshape((hi - lo) * 8, cols)
+        placed = row_hot[:, 8 * lo : 8 * hi]
         for piece in split(got):
             sums = sums + dot(placed, piece)
     surf_v[...] = sums.reshape(4, ATM_ROWS, cols) * share

time: 27.6 us -> 27.2 us (0.986)
  Pallas kernels: 26.8 us -> 26.4 us
    pallas_call x1, Pallas kernels: 25.7 us -> 25.4 us  [local(): pl.pallas_call(functools.partial(kernel, n_lon, n_lat, levels, rows, cols...]
where the time goes in v6:
time: 27.2 us; the launch traced here: 27 us
  Pallas kernels  26.4 us (97%)
  between operations  0.64 us (2%)
    pallas_call x1, Pallas kernels, local(): pl.pallas_call(functools.partial(kernel, n_lon, n_lat, levels, rows, cols...  25.4 us
    pallas_call x1, Pallas kernels, local(): pl.pallas_call(write_out, out_shape=(jax.ShapeDtypeStruct(tracers.shape,...  1.04 us

profile of v6, /device:TPU:1, one launch (start us, length us, event | category | flops | bytes accessed | tf_op | source)
XLA Modules:
  0.0 27.0 jit_solution(13641096136753592455)
XLA Ops:
  0.6 25.4 %ocean.1 = (f32[16,4,32,128]{3,2,1,0:T(8,128)S(1)}, f32[4,32,128]{2,1,0:T(8,128)S(1)}, f32[32,128]{1,0:T(8,128)S(1)}) custom-call(f32[2,16,32,128]{3,2,1,0:T(8,128)} %tracers.1, f32[2,16,32,128]{3,2,1,0:T(8,128)} %velocity.1, s32[32,128]{1,0:T(8,128)} %land_mask.1, f32[32,128]{1,0:T(8,128)} %mixing.1, s32[1,32]{1,0:T(1,128)} %bitcast.2, s32[1,32]{1,0:T(1,128)} %bitcast.3), custom_call_target="tpu_custom_call" | custom-call | tf_op jit(solution)/shard_map/ocean/pallas_call | solution.py:688
  26.0 1.0 %write_out.1 = (f32[2,16,32,128]{3,2,1,0:T(8,128)}, f32[2,16,32,128]{3,2,1,0:T(8,128)}, f32[4,32,128]{2,1,0:T(8,128)}, f32[32,128]{1,0:T(8,128)}) custom-call(f32[16,4,32,128]{3,2,1,0:T(8,128)S(1)} %get-tuple-element.7.x2, f32[4,32,128]{2,1,0:T(8,128)S(1)} %get-tuple-element.8.surf_v, f32[32,128]{1,0:T(8,128)S(1)} %get-tuple-element.9.cover_v), custom_call_target="tpu_custom_call" | custom-call | tf_op jit(solution)/shard_map/write_out/pallas_call | solution.py:696

commit v7 on v6

--- a/solution.py
+++ b/solution.py
@@ -292,7 +292,7 @@
     rim_row = jnp.where(iota((8, cols), 0) < 4, lat * rows - 1, lax.min((lat + 1) * rows, n_lat * rows - 1))
     coriolis8 = turning(rim_row)
 
-    near = devices // 8 * 7
+    near = devices // 16 * 15
 
     def exchange(out, into, sem, height):
         for slot, (a, c) in enumerate(offsets):

time: 27.2 us -> 27.3 us (level)
  no operation moved by 1% of the time
where the time goes in v7:
time: 27.3 us; the launch traced here: 27.1 us
  Pallas kernels  26.5 us (97%)
  between operations  0.64 us (2%)
    pallas_call x1, Pallas kernels, local(): pl.pallas_call(functools.partial(kernel, n_lon, n_lat, levels, rows, cols...  25.4 us
    pallas_call x1, Pallas kernels, local(): pl.pallas_call(write_out, out_shape=(jax.ShapeDtypeStruct(tracers.shape,...  1.04 us

profile of v7, /device:TPU:1, one launch (start us, length us, event | category | flops | bytes accessed | tf_op | source)
XLA Modules:
  0.0 27.1 jit_solution(13669608160801664419)
XLA Ops:
  0.6 25.4 %ocean.1 = (f32[16,4,32,128]{3,2,1,0:T(8,128)S(1)}, f32[4,32,128]{2,1,0:T(8,128)S(1)}, f32[32,128]{1,0:T(8,128)S(1)}) custom-call(f32[2,16,32,128]{3,2,1,0:T(8,128)} %tracers.1, f32[2,16,32,128]{3,2,1,0:T(8,128)} %velocity.1, s32[32,128]{1,0:T(8,128)} %land_mask.1, f32[32,128]{1,0:T(8,128)} %mixing.1, s32[1,32]{1,0:T(1,128)} %bitcast.2, s32[1,32]{1,0:T(1,128)} %bitcast.3), custom_call_target="tpu_custom_call" | custom-call | tf_op jit(solution)/shard_map/ocean/pallas_call | solution.py:688
  26.1 1.0 %write_out.1 = (f32[2,16,32,128]{3,2,1,0:T(8,128)}, f32[2,16,32,128]{3,2,1,0:T(8,128)}, f32[4,32,128]{2,1,0:T(8,128)}, f32[32,128]{1,0:T(8,128)}) custom-call(f32[16,4,32,128]{3,2,1,0:T(8,128)S(1)} %get-tuple-element.7.x2, f32[4,32,128]{2,1,0:T(8,128)S(1)} %get-tuple-element.8.surf_v, f32[32,128]{1,0:T(8,128)S(1)} %get-tuple-element.9.cover_v), custom_call_target="tpu_custom_call" | custom-call | tf_op jit(solution)/shard_map/write_out/pallas_call | solution.py:696
